TPU v7x, 256 devices: a whole 4x4x8 slice. The times are simulated.
256 devices in a mesh: page: 32 (over x, z), tok: 8 (over y, core).
Axes of the slice: x: 4, y: 4, z: 8, core: 2. Of those that a mesh axis runs over, the one named last changes fastest.
Arguments:
- tile_tokens: bfloat16 [32, 4096, 1024], P('page', 'tok'), may hold values from -6 to 6
- page_lengths: int32 [32], P('page'), may hold values from 1 to 4096, as said below
- occupancy: int32 [32, 32], P('page', 'tok'), may hold values 0 or 1
- block_mix: bfloat16 [32, 128, 128], P('tok'), may hold values from -0.5 to 0.5
- stride_mix: bfloat16 [128, 32, 32], P('tok'), may hold values from -1 to 1
- w_gate_up: bfloat16 [2, 1024, 2048], P(None, None, ('page', 'tok')), may hold values from -0.1875 to 0.1875
- w_down: bfloat16 [2048, 1024], P(None, ('page', 'tok')), may hold values from -0.125 to 0.125
Outputs:
- packed_lanes: bfloat16 [8, 16384, 1024], P('tok', 'page')
Inputs may be any that keep to these rules, and one draw needn't show every extreme that they name: `page_lengths`: some page has exactly 4096 used tokens in every draw; page 0 has fewer than 512 used tokens in every draw.
All inputs are finite; a program needn't handle non-finite values. No bound on the sum of `occupancy` on one device may be relied on, other than what follows from the above.
Results may differ from a plain program's by a relative error of at most 0.012.
Values may be sent and summed in bfloat16 or wider, within the bound.
A program may use at most 64 MiB of HBM per device.

v0:
```python
import jax
import jax.numpy as jnp
from jax import lax
from jax.sharding import PartitionSpec as P

epsilon = 1e-05


def entering(value, axis, join, neutral):
    count, mine = (lax.axis_size(axis), lax.axis_index(axis))
    pieces = lax.all_gather(value, axis)
    so_far = jnp.full_like(value, 0) + jnp.asarray(neutral, value.dtype)

    def hop(position, so_far):
        longer = join(so_far, pieces[position])
        return jnp.where(position < mine, longer, so_far)

    return lax.fori_loop(0, count - 1, hop, so_far)


def from_behind(value, axis, by):
    length = lax.axis_size(axis)
    pairs = [(i, i + by) for i in range(length) if 0 <= i + by < length]
    return lax.ppermute(value, axis, pairs)


def rms_round(values):
    scale = lax.rsqrt(jnp.mean(values * values, axis=-1, keepdims=True) + epsilon)
    return (values * scale).astype(jnp.bfloat16)


def add_counts(earlier, later):
    return earlier + later


def channel_mlp(mixed, w_gate_up, w_down):
    mixed_float = mixed.astype(jnp.float32)
    normed_two = rms_round(mixed_float)
    shard_part = lax.all_gather(w_gate_up, ("page", "tok"), axis=2, tiled=True)
    gate_vals = jnp.dot(normed_two, shard_part[0], preferred_element_type=jnp.float32)
    up_vals = jnp.dot(normed_two, shard_part[1], preferred_element_type=jnp.float32)
    hidden = (jax.nn.silu(gate_vals) * up_vals).astype(jnp.bfloat16)
    down_vals = jnp.dot(
        hidden,
        lax.all_gather(w_down, ("page", "tok"), axis=1, tiled=True),
        preferred_element_type=jnp.float32,
    )
    return (mixed_float + down_vals).astype(jnp.bfloat16)


def lane_relay(row_data, length, lane_index):
    row_count = row_data.shape[0]
    page_here = lax.axis_index("page")
    live_rows = jnp.clip(length - lane_index * row_count, 0, row_count)
    before = entering(live_rows.reshape(1), "page", add_counts, jnp.zeros((1,), jnp.int32))[0]
    distance = page_here * row_count - before
    in_shift = distance % row_count
    hop_count = distance // row_count
    row_ids = jnp.arange(row_count, dtype=jnp.int32)
    live_flag = row_ids < live_rows
    kept_data = jnp.where(live_flag[:, None], row_data, jnp.zeros_like(row_data))
    kept_tags = jnp.where(live_flag, hop_count + 1, 0).astype(jnp.int32)
    zero_data = jnp.zeros_like(row_data)
    zero_tags = jnp.zeros_like(kept_tags)
    here_data = lax.dynamic_slice_in_dim(
        jnp.concatenate([kept_data, zero_data], 0), in_shift, row_count, 0
    )
    here_tags = lax.dynamic_slice_in_dim(
        jnp.concatenate([kept_tags, zero_tags], 0), in_shift, row_count, 0
    )
    spill_data = lax.dynamic_slice_in_dim(
        jnp.concatenate([zero_data, kept_data], 0), in_shift, row_count, 0
    )
    spill_tags = lax.dynamic_slice_in_dim(
        jnp.concatenate([zero_tags, kept_tags], 0), in_shift, row_count, 0
    )
    got_data, got_tags = from_behind((spill_data, spill_tags), "page", -1)
    arrived = got_tags > 0
    cur_data = jnp.where(arrived[:, None], got_data, here_data)
    cur_tags = jnp.where(arrived, got_tags, here_tags)
    for bit_pos in range((lax.axis_size("page") - 1).bit_length()):
        stride_len = 1 << bit_pos
        present = cur_tags > 0
        moving = present & ((cur_tags - 1) // stride_len % 2 == 1)
        staying = present & jnp.logical_not(moving)
        out_data = jnp.where(moving[:, None], cur_data, jnp.zeros_like(cur_data))
        out_tags = jnp.where(moving, cur_tags, 0)
        got_data, got_tags = from_behind((out_data, out_tags), "page", -stride_len)
        arrived = got_tags > 0
        kept_now = jnp.where(staying[:, None], cur_data, jnp.zeros_like(cur_data))
        cur_data = jnp.where(arrived[:, None], got_data, kept_now)
        cur_tags = jnp.where(arrived, got_tags, jnp.where(staying, cur_tags, 0))
    return cur_data


def per_device(tile_tokens, page_lengths, occupancy, block_mix, stride_mix, w_gate_up, w_down):
    lane_index = lax.axis_index("tok")
    row_count = tile_tokens.shape[1]
    feat_width = tile_tokens.shape[2]
    blocks_here = block_mix.shape[0]
    blk_size = block_mix.shape[1]
    length = page_lengths[0]
    positions = lane_index * row_count + jnp.arange(row_count, dtype=jnp.int32)
    live_mask = (positions < length) & (jnp.repeat(occupancy[0], blk_size) > 0)
    masked = jnp.where(live_mask[:, None], tile_tokens[0].astype(jnp.float32), 0.0)
    normed = rms_round(masked).reshape(blocks_here, blk_size, feat_width)
    first = jnp.einsum(
        "bji,bic->bjc", block_mix, normed, preferred_element_type=jnp.float32
    ).astype(jnp.bfloat16)
    second = jnp.einsum(
        "jkb,bjc->jkc",
        stride_mix,
        lax.all_to_all(first, "tok", split_axis=1, concat_axis=0, tiled=True),
        preferred_element_type=jnp.float32,
    )
    mixed = (masked + second.reshape(row_count, feat_width)).astype(jnp.bfloat16)
    layer_out = channel_mlp(mixed, w_gate_up, w_down)
    packed = lane_relay(layer_out, length, lane_index)
    return packed.reshape(1, row_count, feat_width)


def solution(mesh):
    return jax.shard_map(
        per_device,
        mesh=mesh,
        in_specs=(
            P("page", "tok", None),
            P("page"),
            P("page", "tok"),
            P("tok", None, None),
            P("tok", None, None),
            P(None, None, ("page", "tok")),
            P(None, ("page", "tok")),
        ),
        out_specs=P("tok", "page", None),
        check_vma=False,
    )
```

profile of v0, /device:TPU:224, one launch (start us, length us, event | category | flops | bytes accessed | tf_op | source)
XLA Modules:
  0.0 485.3 jit_solution(8007131997813396704)
XLA Ops:
  6.5 0.7 all-gather.6.cloned.1.call-update
  7.3 0.7 all-gather.4.cloned.1.call-update
  8.7 1.5 convert_element_type.76
  10.2 1.8 copy.13
  12.6 3.0 fusion.7
  15.6 2.7 copy.14
  18.3 4.5 all-to-all-start
  23.4 0.7 dynamic-update-slice
  24.1 16.0 %all-reduce.4 = s32[32]{0:T(128)S(1)} all-reduce(s32[32]{0:T(128)S(1)} %dynamic-update-slice), channel_id=1, replica_groups=mesh['page'=32,'tok'=8] {'page'}, use_global_device_ids=true, to_apply=%add.4 | all-reduce | flops 32 | bytes 256
  40.1 42.9 %while.13 = (s32[]{:T(128)}, s32[1]{0:T(128)}, s32[]{:T(128)}, s32[32,1]{0,1:T(1,128)S(1)}, s32[]{:T(128)}) while((s32[]{:T(128)}, s32[1]{0:T(128)}, s32[]{:T(128)}, s32[32,1]{0,1:T(1,128)S(1)}, s32[]{:T(128)}) %tuple.53), condition=%wide.region_1.2_spmd, body=%wide.region_0.1_spmd.sunk | while | flops 5 | bytes 115 | solution.py:18
  41.5 0.7 constant_dynamic-slice_fusion.2
  42.9 0.7 constant_dynamic-slice_fusion.2
  44.3 0.7 constant_dynamic-slice_fusion.2
  45.6 0.7 constant_dynamic-slice_fusion.2
  48.4 0.7 constant_dynamic-slice_fusion.2
  49.8 0.7 constant_dynamic-slice_fusion.2
  51.2 0.7 constant_dynamic-slice_fusion.2
  52.6 0.7 constant_dynamic-slice_fusion.2
  54.0 0.7 constant_dynamic-slice_fusion.2
  56.7 0.7 constant_dynamic-slice_fusion.2
  58.1 0.7 constant_dynamic-slice_fusion.2
  59.5 0.7 constant_dynamic-slice_fusion.2
  60.9 0.7 constant_dynamic-slice_fusion.2
  63.7 0.7 constant_dynamic-slice_fusion.2
  65.0 0.7 constant_dynamic-slice_fusion.2
  66.4 0.7 constant_dynamic-slice_fusion.2
  67.8 0.7 constant_dynamic-slice_fusion.2
  69.2 0.7 constant_dynamic-slice_fusion.2
  72.0 0.7 constant_dynamic-slice_fusion.2
  73.4 0.7 constant_dynamic-slice_fusion.2
  74.7 0.7 constant_dynamic-slice_fusion.2
  76.1 0.7 constant_dynamic-slice_fusion.2
  77.5 0.7 constant_dynamic-slice_fusion.2
  80.3 0.7 constant_dynamic-slice_fusion.2
  83.3 1.5 copy.15
  84.9 1.8 copy.16
  86.6 2.2 all_to_all.16
  88.8 1.8 fusion.2
  91.3 33.8 %all-gather.6.cloned.1.call-done = bf16[256,4,2048]{2,1,0:T(4,128)(2,1)} async-done(((bf16[1,4,2048]{2,1,0:T(4,128)(2,1)}), bf16[256,4,2048]{2,1,0:T(4,128)(2,1)}) %all-gather.6.cloned.1.call-update) | async-done | bytes 4194320 | tf_op jit(solution)/shard_map/all_gather | solution.py:45
  125.0 6.9 %reshape.137 = bf16[1024,2048]{1,0:T(8,128)(2,1)} reshape(bf16[256,4,2048]{2,1,0:T(4,128)(2,1)} %all-gather.6.cloned.1.call-done) | data formatting | bytes 8388608
  131.9 111.8 %all-gather.4.cloned.1.call-done = bf16[2,1024,2048]{1,2,0:T(8,128)(2,1)} async-done(((bf16[2,1024,8]{1,2,0:T(8,128)(2,1)}), bf16[2,1024,2048]{1,2,0:T(8,128)(2,1)}) %all-gather.4.cloned.1.call-update) | async-done | bytes 8388624 | tf_op jit(solution)/shard_map/all_gather | solution.py:39
  243.7 6.5 %fusion.1 = f32[512,2048]{1,0:T(8,128)} fusion(bf16[512,1024]{1,0:T(8,128)(2,1)S(1)} %bitcast.75, bf16[2,1024,2048]{1,2,0:T(8,128)(2,1)} %all-gather.4.cloned.1.call-done), kind=kOutput, calls=%fused_computation.4 | convolution fusion | flops 2147483648 | bytes 9437184 | tf_op jit(solution)/shard_map/dot_general | solution.py:40
  250.3 9.2 %fusion.8 = bf16[512,1024]{1,0:T(8,128)(2,1)S(1)} fusion(bf16[1024,2048]{1,0:T(8,128)(2,1)} %reshape.137, f32[512,2048]{1,0:T(8,128)} %fusion.1, bf16[512,1024]{1,0:T(8,128)(2,1)S(1)} %bitcast.76, bf16[2,1024,2048]{1,2,0:T(8,128)(2,1)} %all-gather.4.cloned.1.call-done, bf16[512,1024]{1,0:T(8,128)(2,1)S(1)} %fusion.4, pred[512]{0:T(512)(128)(4,1)S(1)} %iota_compare_fusion), kind=kOutput, calls=%fused_computation.23 | convolution fusion | flops 4303355904 | bytes 15729152 | tf_op jit(solution)/shard_map/dot_general | solution.py:43
  259.5 0.7 pad_dynamic-slice_fusion.1
  260.2 3.1 collective-permute-start.6
  263.4 2.3 collective-permute-start
  265.7 23.9 %collective-permute-done = s32[512]{0:T(512)S(1)} collective-permute-done((s32[512]{0:T(512)S(1)}, s32[512]{0:T(512)S(1)}, u32[]{:S(2)}, u32[]{:S(2)}) %collective-permute-start) | collective-permute-done | bytes 2080 | tf_op jit(solution)/shard_map/ppermute | solution.py:24
  290.3 1.9 collective-permute-start.7
  292.2 1.9 collective-permute-start.1
  294.1 24.7 %collective-permute-done.1 = s32[512]{0:T(512)S(1)} collective-permute-done((s32[512]{0:T(512)S(1)}, s32[512]{0:T(512)S(1)}, u32[]{:S(2)}, u32[]{:S(2)}) %collective-permute-start.1) | collective-permute-done | bytes 2080 | tf_op jit(solution)/shard_map/ppermute | solution.py:24
  318.9 1.2 broadcast_select_fusion.1
  320.1 1.9 collective-permute-start.8
  322.0 3.6 collective-permute-start.2
  325.6 43.7 %collective-permute-done.2 = s32[512]{0:T(512)S(1)} collective-permute-done((s32[512]{0:T(512)S(1)}, s32[512]{0:T(512)S(1)}, u32[]{:S(2)}, u32[]{:S(2)}) %collective-permute-start.2) | collective-permute-done | bytes 2080 | tf_op jit(solution)/shard_map/ppermute | solution.py:24
  369.6 1.9 collective-permute-start.9
  371.5 1.9 collective-permute-start.3
  373.5 48.2 %collective-permute-done.3 = s32[512]{0:T(512)S(1)} collective-permute-done((s32[512]{0:T(512)S(1)}, s32[512]{0:T(512)S(1)}, u32[]{:S(2)}, u32[]{:S(2)}) %collective-permute-start.3) | collective-permute-done | bytes 2080 | tf_op jit(solution)/shard_map/ppermute | solution.py:24
  422.3 1.3 collective-permute-start.10
  423.6 1.3 collective-permute-start.4
  424.9 24.4 %collective-permute-done.4 = s32[512]{0:T(512)S(1)} collective-permute-done((s32[512]{0:T(512)S(1)}, s32[512]{0:T(512)S(1)}, u32[]{:S(2)}, u32[]{:S(2)}) %collective-permute-start.4) | collective-permute-done | bytes 2080 | tf_op jit(solution)/shard_map/ppermute | solution.py:24
  449.7 1.3 collective-permute-start.11
  451.0 1.3 collective-permute-start.5
  452.3 24.7 %collective-permute-done.5 = s32[512]{0:T(512)S(1)} collective-permute-done((s32[512]{0:T(512)S(1)}, s32[512]{0:T(512)S(1)}, u32[]{:S(2)}, u32[]{:S(2)}) %collective-permute-start.5) | collective-permute-done | bytes 2080 | tf_op jit(solution)/shard_map/ppermute | solution.py:24
  477.0 1.5 select_bitcast_fusion
  (58 shorter events, 8.9 us)
Async XLA Ops:
  6.5 82.3 %copy-start = (bf16[16,32,32]{2,1,0:T(8,128)(2,1)S(1)}, bf16[16,32,32]{2,1,0:T(8,128)(2,1)}, u32[]{:S(2)}) copy-start(bf16[16,32,32]{2,1,0:T(8,128)(2,1)} %param.13) | copy-start | bytes 98308
  6.5 118.5 %all-gather.6.cloned.1.call-start = ((), (), s32[]{:S(2)}) async-start(), calls=%async_computation.2 | async-start | bytes 4210688 | tf_op jit(solution)/shard_map/all_gather | solution.py:45
  7.3 236.5 %all-gather.4.cloned.1.call-start = ((), (), s32[]{:S(2)}) async-start(), calls=%async_computation.1 | async-start | bytes 8421376 | tf_op jit(solution)/shard_map/all_gather | solution.py:39
  10.1 1.9 copy-start.3
  10.1 1.9 copy-start.1
  10.2 2.4 copy-start.2
  15.6 7.1 %copy-start.4 = (u32[256]{0:T(256)S(1)}, u32[256]{0:T(256)}, u32[]{:S(2)}) copy-start(u32[256]{0:T(256)} %constant.185) | copy-start | bytes 3076
  18.3 65.0 %all-to-all-start = ((bf16[4,128,1024]{2,0,1:T(4,128)(2,1)}), bf16[4,128,1024]{2,0,1:T(4,128)(2,1)}, u32[]{:S(2)}, u32[]{:S(2)}) async-start(bf16[4,128,1024]{2,0,1:T(4,128)(2,1)} %copy.14), calls=%async_computation | async-start | bytes 2097152 | tf_op jit(solution)/shard_map/all_to_all | solution.py:113
  260.2 29.5 %collective-permute-start.6 = (bf16[512,1024]{1,0:T(8,128)(2,1)S(1)}, bf16[512,1024]{1,0:T(8,128)(2,1)S(1)}, u32[]{:S(2)}, u32[]{:S(2)}) collective-permute-start(bf16[512,1024]{1,0:T(8,128)(2,1)S(1)} %pad_dynamic-slice_fusion.1), channel_id=1, source_target_pairs={{8,0},{16,8},{24,16},{32,24},{40,32},{48,40},{56,48},{64,56},{72,6... | collective-permute-start | bytes 3145736 | tf_op jit(solution)/shard_map/ppermute | solution.py:24
  263.4 26.2 %collective-permute-start = (s32[512]{0:T(512)S(1)}, s32[512]{0:T(512)S(1)}, u32[]{:S(2)}, u32[]{:S(2)}) collective-permute-start(s32[512]{0:T(512)S(1)} %pad_dynamic-slice_fusion.3), channel_id=1, source_target_pairs={{8,0},{16,8},{24,16},{32,24},{40,32},{48,40},{56,48},{64,56},{72,6... | collective-permute-start | bytes 6152 | tf_op jit(solution)/shard_map/ppermute | solution.py:24
  290.3 28.6 %collective-permute-start.7 = (bf16[512,1024]{1,0:T(8,128)(2,1)S(1)}, bf16[512,1024]{1,0:T(8,128)(2,1)S(1)}, u32[]{:S(2)}, u32[]{:S(2)}) collective-permute-start(bf16[512,1024]{1,0:T(8,128)(2,1)S(1)} %broadcast_select_fusion), channel_id=1, source_target_pairs={{8,0},{16,8},{24,16},{32,24},{40,32},{48,40},{56,48},{64,56},{72,6... | collective-permute-start | bytes 3145736 | tf_op jit(solution)/shard_map/ppermute | solution.py:24
  292.2 26.6 %collective-permute-start.1 = (s32[512]{0:T(512)S(1)}, s32[512]{0:T(512)S(1)}, u32[]{:S(2)}, u32[]{:S(2)}) collective-permute-start(s32[512]{0:T(512)S(1)} %broadcast_select_fusion.9), channel_id=1, source_target_pairs={{8,0},{16,8},{24,16},{32,24},{40,32},{48,40},{56,48},{64,56},{72,6... | collective-permute-start | bytes 6152 | tf_op jit(solution)/shard_map/ppermute | solution.py:24
  320.1 49.2 %collective-permute-start.8 = (bf16[512,1024]{1,0:T(8,128)(2,1)S(1)}, bf16[512,1024]{1,0:T(8,128)(2,1)S(1)}, u32[]{:S(2)}, u32[]{:S(2)}) collective-permute-start(bf16[512,1024]{1,0:T(8,128)(2,1)S(1)} %get-tuple-element.107), channel_id=1, source_target_pairs={{16,0},{24,8},{32,16},{40,24},{48,32},{56,40},{64,48},{72,56},{80,... | collective-permute-start | bytes 3145736 | tf_op jit(solution)/shard_map/ppermute | solution.py:24
  322.0 47.3 %collective-permute-start.2 = (s32[512]{0:T(512)S(1)}, s32[512]{0:T(512)S(1)}, u32[]{:S(2)}, u32[]{:S(2)}) collective-permute-start(s32[512]{0:T(512)S(1)} %broadcast_select_fusion.7), channel_id=1, source_target_pairs={{16,0},{24,8},{32,16},{40,24},{48,32},{56,40},{64,48},{72,56},{80,... | collective-permute-start | bytes 6152 | tf_op jit(solution)/shard_map/ppermute | solution.py:24
  369.6 52.1 %collective-permute-start.9 = (bf16[512,1024]{1,0:T(8,128)(2,1)S(1)}, bf16[512,1024]{1,0:T(8,128)(2,1)S(1)}, u32[]{:S(2)}, u32[]{:S(2)}) collective-permute-start(bf16[512,1024]{1,0:T(8,128)(2,1)S(1)} %broadcast_select_fusion.2), channel_id=1, source_target_pairs={{32,0},{40,8},{48,16},{56,24},{64,32},{72,40},{80,48},{88,56},{96,... | collective-permute-start | bytes 3145736 | tf_op jit(solution)/shard_map/ppermute | solution.py:24
  371.5 50.1 %collective-permute-start.3 = (s32[512]{0:T(512)S(1)}, s32[512]{0:T(512)S(1)}, u32[]{:S(2)}, u32[]{:S(2)}) collective-permute-start(s32[512]{0:T(512)S(1)} %broadcast_select_fusion.5), channel_id=1, source_target_pairs={{32,0},{40,8},{48,16},{56,24},{64,32},{72,40},{80,48},{88,56},{96,... | collective-permute-start | bytes 6152 | tf_op jit(solution)/shard_map/ppermute | solution.py:24
  422.3 27.0 %collective-permute-start.10 = (bf16[512,1024]{1,0:T(8,128)(2,1)S(1)}, bf16[512,1024]{1,0:T(8,128)(2,1)S(1)}, u32[]{:S(2)}, u32[]{:S(2)}) collective-permute-start(bf16[512,1024]{1,0:T(8,128)(2,1)S(1)} %get-tuple-element.99), channel_id=1, source_target_pairs={{64,0},{72,8},{80,16},{88,24},{96,32},{104,40},{112,48},{120,56},{... | collective-permute-start | bytes 3145736 | tf_op jit(solution)/shard_map/ppermute | solution.py:24
  423.6 25.7 %collective-permute-start.4 = (s32[512]{0:T(512)S(1)}, s32[512]{0:T(512)S(1)}, u32[]{:S(2)}, u32[]{:S(2)}) collective-permute-start(s32[512]{0:T(512)S(1)} %broadcast_select_fusion.8), channel_id=1, source_target_pairs={{64,0},{72,8},{80,16},{88,24},{96,32},{104,40},{112,48},{120,56},{... | collective-permute-start | bytes 6152 | tf_op jit(solution)/shard_map/ppermute | solution.py:24
  449.7 27.3 %collective-permute-start.11 = (bf16[512,1024]{1,0:T(8,128)(2,1)S(1)}, bf16[512,1024]{1,0:T(8,128)(2,1)S(1)}, u32[]{:S(2)}, u32[]{:S(2)}) collective-permute-start(bf16[512,1024]{1,0:T(8,128)(2,1)S(1)} %broadcast_select_fusion.4), channel_id=1, source_target_pairs={{128,0},{136,8},{144,16},{152,24},{160,32},{168,40},{176,48},{184,... | collective-permute-start | bytes 3145736 | tf_op jit(solution)/shard_map/ppermute | solution.py:24
  451.0 26.0 %collective-permute-start.5 = (s32[512]{0:T(512)S(1)}, s32[512]{0:T(512)S(1)}, u32[]{:S(2)}, u32[]{:S(2)}) collective-permute-start(s32[512]{0:T(512)S(1)} %get-tuple-element.93), channel_id=1, source_target_pairs={{128,0},{136,8},{144,16},{152,24},{160,32},{168,40},{176,48},{184,... | collective-permute-start | bytes 6152 | tf_op jit(solution)/shard_map/ppermute | solution.py:24
Sparse Core Ops, SparseCore 0:
  11.0 113.9 all-gather.5
  128.7 115.0 all-gather.3
where the time goes:
time: 486 us; the launch traced here: 485 us
  waiting for transfers between devices  337 us (69%)
  local copies, waits for them, and re-layouts  39.8 us (8%)
  starting transfers between devices  28.2 us (6%)
  loops' own time  22.3 us (5%)
  matrix products  20.6 us (4%)
  blocking collectives  16 us (3%)
  between operations  14.4 us (3%)
  other arithmetic  7.44 us (2%)
    ppermute x12, waiting for transfers between devices, from_behind(): return lax.ppermute(value, axis, pairs)  189 us
    all_gather x1, waiting for transfers between devices, channel_mlp(): shard_part = lax.all_gather(w_gate_up, ('page', 'tok'), axis=2, tiled=True)  112 us
    all_gather x1, waiting for transfers between devices, channel_mlp(): lax.all_gather(w_down, ('page', 'tok'), axis=1, tiled=True)  33.8 us
    ppermute x12, starting transfers between devices, from_behind(): return lax.ppermute(value, axis, pairs)  23.7 us
    another operation x1, loops' own time, entering(): return lax.fori_loop(0, count - 1, hop, so_far)  22.3 us
    dynamic_slice x31, local copies, waits for them, and re-layouts, hop(): longer = join(so_far, pieces[position])  20.6 us
    unnamed x1, blocking collectives  16 us
  transfers between devices with their start and end apart: 15, of which 8 were waited for; matrix products, arithmetic and copies ran while one was open for 9% of the time, Pallas kernels for 0%

commit v1 on v0

v1 whole, which is shorter than its diff:
```python
import jax
import jax.numpy as jnp
from jax import lax
from jax.experimental import pallas as pl
from jax.experimental.pallas import tpu as pltpu
from jax.sharding import PartitionSpec as P

NX, NZ, NY, NC = 4, 8, 4, 2
PAGES, TOKS = 32, 8
ROWS, D, FF = 512, 1024, 2048
BLK, NB, PER = 128, 32, 16
EPS = 1e-05
MESH = pl.DeviceIdType.MESH
NT = (((1,), (1,)), ((), ()))
BF, F32 = jnp.bfloat16, jnp.float32


def mod(a, n):
    return lax.rem(a, jnp.int32(n))


def div(a, n):
    return lax.div(a, jnp.int32(n))


def iota(shape, dim):
    return lax.broadcasted_iota(jnp.int32, shape, dim)


def matmul(a, b):
    return jnp.dot(a, b, preferred_element_type=F32)


def matmul_nt(a, b):
    return lax.dot_general(a, b, NT, preferred_element_type=F32)


def rms_round(values):
    scale = lax.rsqrt(jnp.mean(values * values, axis=-1, keepdims=True) + EPS)
    return (values * scale).astype(BF)


def body(
    len_ref, occ_ref, x_ref, bm_ref, sm_ref, wg_ref, wd_ref, o_ref,
    lens_rx, gu_tx, gu_rx, wd_tx, wd_rx, w, fsend, frecv, xm, spread, pre, psel,
    p1tx, p1rx, ymix, ynorm, hid, p2tx,
    lens_s, lens_r, gu_s, gu_r, wd_s, wd_r, z_s, z_r, tok_s, tok_r,
    p1_s, p1_r, p2_s, p2_r, ring_s, ring_r, core_s, core_r, own_s,
):
    page, tok = lax.axis_index("page"), lax.axis_index("tok")
    x, z = div(page, NZ), mod(page, NZ)
    y, c = div(tok, NC), mod(tok, NC)
    yh, yl = div(y, 2), mod(y, 2)
    sibling = tok + 1 - 2 * c

    def rcopy(src, dst, ssem, rsem, to_page, to_tok):
        return pltpu.make_async_remote_copy(
            src_ref=src, dst_ref=dst, send_sem=ssem, recv_sem=rsem,
            device_id=(to_page, to_tok), device_id_type=MESH,
        )

    def wait_recv(ref, sem):
        rcopy(ref, ref, sem, sem, page, sibling).wait_recv()

    def wait_send(ref, sem):
        rcopy(ref, ref, sem, sem, page, sibling).wait_send()

    barrier = pltpu.get_barrier_semaphore()

    @pl.loop(1, PAGES)
    def _(k):
        pl.semaphore_signal(barrier, inc=1, device_id=(mod(page + k, PAGES), tok), device_id_type=MESH)

    @pl.loop(1, TOKS)
    def _(k):
        pl.semaphore_signal(barrier, inc=1, device_id=(page, mod(tok + k, TOKS)), device_id_type=MESH)

    length = len_ref[0]
    place8 = (iota((16, 8), 0) == iota((16, 8), 1) + 8 * c).astype(BF)
    place4 = (iota((16, 4), 0) == iota((16, 4), 1) + 4 * mod(tok, 4)).astype(BF)
    for g in range(2):
        gu_tx[g] = matmul(place8, wg_ref[g]).astype(BF)
    wd_all = matmul(place4, wd_ref[...]).astype(BF)
    for q in range(4):
        wd_tx[q] = wd_all[:, q * 512 : (q + 1) * 512]
    lens_rx[page] = jnp.full((8, 128), length, jnp.int32)

    pl.semaphore_wait(barrier, PAGES - 1 + TOKS - 1)

    rcopy(gu_tx.at[1 - c], gu_rx, gu_s, gu_r, page, sibling).start()
    half = 4 * div(tok, 4)
    for k in range(1, 4):
        q = mod(tok + k, 4)
        rcopy(wd_tx.at[q], wd_rx.at[3 - k], wd_s, wd_r, page, half + q).start()

    @pl.loop(1, PAGES)
    def _(k):
        rcopy(lens_rx.at[page], lens_rx.at[page], lens_s, lens_r, mod(page + k, PAGES), tok).start()

    for b in range(4):
        limit = length * occ_ref[0, b] - tok * ROWS - b * BLK
        rows = slice(b * BLK, (b + 1) * BLK)
        live = iota((BLK, D), 0) < limit
        masked = jnp.where(live, x_ref[rows, :].astype(F32), 0.0)
        xm[rows, :] = masked.astype(BF)
        first = matmul(bm_ref[b], rms_round(masked)).astype(BF)
        fsend[:, b] = first.reshape(TOKS, PER, D)

    @pl.loop(1, TOKS)
    def _(k):
        to = mod(tok + k, TOKS)
        rcopy(fsend.at[to], frecv.at[tok], tok_s, tok_r, page, to).start()

    own_first = pltpu.make_async_copy(fsend.at[tok], frecv.at[tok], own_s.at[0])
    own_first.start()

    wait_recv(gu_rx, gu_r)
    wait_recv(wd_rx, wd_r)
    w[c, x, z, yh, yl, :, 0:D] = gu_tx[c] + gu_rx[...]
    w[c, x, z, yh, yl, :, D:] = wd_tx[mod(tok, 4)] + wd_rx[0] + wd_rx[1] + wd_rx[2]

    @pl.loop(1, NZ)
    def _(k):
        unit = w.at[c, x, z, yh, yl]
        rcopy(unit, unit, z_s, z_r, x * NZ + mod(z + k, NZ), tok).start()

    expand = (iota((NB, ROWS), 0) == iota((NB, ROWS), 1) // PER).astype(BF)
    wide = matmul(sm_ref[...].reshape(ROWS, NB), expand)
    same = iota((ROWS, ROWS), 1) % PER == iota((ROWS, ROWS), 0) // 32
    spread[...] = jnp.where(same, wide, 0.0).astype(BF)

    wait_recv(lens_rx.at[pl.ds(0, PAGES - 1)], lens_r)
    lens = lens_rx[:, 0, :]
    lens = jnp.concatenate([lens] * 4, axis=1)
    kept = jnp.clip(lens - tok * ROWS, 0, ROWS)
    who = iota((PAGES, ROWS), 0)
    lane_page = iota((PAGES, ROWS), 1) // PER
    shift = jnp.sum(jnp.where(who < page, kept, 0), axis=0, keepdims=True)
    start_of = jnp.sum(jnp.where(who < lane_page, kept, 0), axis=0, keepdims=True)
    stop_of = start_of + jnp.sum(jnp.where(who == lane_page, kept, 0), axis=0, keepdims=True)

    @pl.loop(0, 4)
    def _(r):
        rows = pl.ds(pl.multiple_of(r * 128, 128), 128)
        slot = iota((128, ROWS), 0) + r * 128
        turn = (((iota((128, ROWS), 1) + shift) & (ROWS - 1)) == slot).astype(BF)
        pre[rows, :] = matmul(turn, xm[...]).astype(BF)
        psel[rows, :] = matmul(turn, spread[...]).astype(BF)

    def ylo(yy, z0, n):
        return w.at[c, :, pl.ds(z0, n), div(yy, 2), mod(yy, 2)]

    def xhi(xx, z0, n):
        return w.at[c, xx, pl.ds(z0, n)]

    def xlo(xx, z0, n):
        return w.at[c, xx, pl.ds(z0, n), yh, yl]

    def yhi(yy, z0, n):
        return w.at[c, x, pl.ds(z0, n), div(yy, 2), mod(yy, 2)]

    def xdev(by):
        return mod(x + by, NX) * NZ + z, tok

    def ydev(by):
        return page, mod(y + by, NY) * NC + c

    rings = [
        [(xlo, x, xdev, 0, NX), (yhi, y, ydev, 4, NY)],
        [(ylo, y, ydev, 0, NY), (xhi, x, xdev, 4, NX)],
    ]

    def ring_copy(stage, which, hop, way):
        piece, me, dev, z0, n = rings[stage][which]
        by = 1 if way == 0 else n - 1
        if hop == 0:
            ref = piece(me, z0, 4)
        else:
            ref = piece(mod(me + n - by, n), z0 + 2 * way, 2)
        i = stage * 8 + hop * 4 + which * 2 + way
        return rcopy(ref, ref, ring_s.at[i], ring_r.at[i], *dev(by))

    def ring_arrived(stage, which, hop, way):
        piece, me, dev, z0, n = rings[stage][which]
        by = 1 if way == 0 else n - 1
        ref = piece(mod(me + n - by, n), z0, 4) if hop == 0 else piece(mod(me + 2, n), z0 + 2 * way, 2)
        wait_recv(ref, ring_r.at[stage * 8 + hop * 4 + which * 2 + way])

    both = [(which, way) for which in range(2) for way in range(2)]

    def core_copy(i, ref):
        copy = rcopy(ref, ref, core_s.at[i], core_r.at[i], page, sibling)
        copy.start()
        return copy

    wait_recv(w.at[c, x, pl.ds(0, NZ - 1), yh, yl], z_r)
    for which, way in both:
        ring_copy(0, which, 0, way).start()
    for which, way in both:
        ring_arrived(0, which, 0, way)
        ring_copy(0, which, 1, way).start()

    own_first.wait()
    wait_recv(frecv.at[pl.ds(0, TOKS - 1)], tok_r)

    @pl.loop(0, 4)
    def _(r):
        rows = pl.ds(pl.multiple_of(r * 128, 128), 128)
        second = matmul(psel[rows, :], frecv[...].reshape(ROWS, D))
        mixed = (pre[rows, :].astype(F32) + second).astype(BF)
        p1tx[pl.ds(r * 8, 8)] = mixed.reshape(8, PER, D)

    @pl.loop(1, PAGES)
    def _(k):
        to = mod(page + k, PAGES)
        rcopy(p1tx.at[to], p1rx.at[page], p1_s, p1_r, to, tok).start()

    own_p1 = pltpu.make_async_copy(p1tx.at[page], p1rx.at[page], own_s.at[1])
    own_p1.start()

    for which, way in both:
        ring_arrived(0, which, 1, way)
    for which, way in both:
        ring_copy(1, which, 0, way).start()
    cores = [core_copy(0, ylo(y, 0, 4)), core_copy(1, xhi(x, 4, 4))]
    for which, way in both:
        ring_arrived(1, which, 0, way)
        ring_copy(1, which, 1, way).start()
        piece, me, dev, z0, n = rings[1][which]
        by = 1 if way == 0 else n - 1
        cores.append(core_copy(2 + 2 * which + way, piece(mod(me + n - by, n), z0, 4)))

    own_p1.wait()
    wait_recv(p1rx.at[pl.ds(0, PAGES - 1)], p1_r)

    @pl.loop(0, 4)
    def _(r):
        rows = pl.ds(pl.multiple_of(r * 128, 128), 128)
        row = iota((128, ROWS), 0) + r * 128
        col = iota((128, ROWS), 1)
        target = (row // PER) * ROWS + page * PER + row % PER
        pick = (row % PER == col % PER) & (target >= start_of) & (target < stop_of)
        mixed = matmul(pick.astype(BF), p1rx[...].reshape(ROWS, D))
        ymix[rows, :] = mixed.astype(BF)
        ynorm[rows, :] = rms_round(mixed)

    for which, way in both:
        ring_arrived(1, which, 1, way)
    cores.append(core_copy(6, ylo(mod(y + 2, NY), 0, 4)))
    cores.append(core_copy(7, xhi(mod(x + 2, NX), 4, 4)))
    for copy in cores:
        copy.wait_recv()

    @pl.loop(0, 8)
    def _(t):
        at = (t // 2, pl.ds(4 * (t % 2), 4))
        gate = matmul_nt(ynorm[...], w[(0, *at, slice(None), slice(None), slice(None), slice(0, D))].reshape(256, D))
        up = matmul_nt(ynorm[...], w[(1, *at, slice(None), slice(None), slice(None), slice(0, D))].reshape(256, D))
        hid[:, pl.ds(pl.multiple_of(t * 256, 256), 256)] = (gate / (1.0 + jnp.exp(-gate)) * up).astype(BF)

    @pl.loop(0, 4)
    def _(t):
        cols = pl.ds(pl.multiple_of(t * 256, 256), 256)
        total = ymix[:, cols].astype(F32)
        for q in range(4):
            down = w[q % 2, t, :, :, q // 2, :, D:].reshape(256, 512)
            total = total + matmul_nt(hid[:, q * 512 : (q + 1) * 512], down)
        p2tx[:, :, cols] = total.astype(BF).reshape(PAGES, PER, 256)

    @pl.loop(1, PAGES)
    def _(k):
        to = mod(page + k, PAGES)
        rcopy(p2tx.at[to], o_ref.at[page], p2_s, p2_r, to, tok).start()

    own_p2 = pltpu.make_async_copy(p2tx.at[page], o_ref.at[page], own_s.at[2])
    own_p2.start()

    wait_send(gu_rx, gu_s)
    wait_send(wd_rx, wd_s)
    wait_send(lens_rx.at[pl.ds(0, PAGES - 1)], lens_s)
    wait_send(w.at[c, x, pl.ds(0, NZ - 1), yh, yl], z_s)
    wait_send(frecv.at[pl.ds(0, TOKS - 1)], tok_s)
    wait_send(p1tx.at[pl.ds(0, PAGES - 1)], p1_s)
    for stage in range(2):
        for hop in range(2):
            for which, way in both:
                ring_copy(stage, which, hop, way).wait_send()
    for copy in cores:
        copy.wait_send()
    own_p2.wait()
    wait_send(p2tx.at[pl.ds(0, PAGES - 1)], p2_s)
    wait_recv(o_ref.at[pl.ds(0, PAGES - 1)], p2_r)


def per_device(tile_tokens, page_lengths, occupancy, block_mix, stride_mix, w_gate_up, w_down):
    vmem = pl.BlockSpec(memory_space=pltpu.VMEM)
    smem = pl.BlockSpec(memory_space=pltpu.SMEM)
    dma = pltpu.SemaphoreType.DMA
    packed = pl.pallas_call(
        body,
        out_shape=jax.ShapeDtypeStruct((PAGES, PER, D), BF),
        in_specs=[smem, smem] + [vmem] * 5,
        out_specs=vmem,
        scratch_shapes=[
            pltpu.VMEM((PAGES, 8, 128), jnp.int32),
            pltpu.VMEM((2, 16, D), BF),
            pltpu.VMEM((16, D), BF),
            pltpu.VMEM((4, 16, 512), BF),
            pltpu.VMEM((3, 16, 512), BF),
            pltpu.VMEM((NC, NX, NZ, 2, 2, 16, D + 512), BF),
            pltpu.VMEM((TOKS, 4, PER, D), BF),
            pltpu.VMEM((TOKS, 4, PER, D), BF),
            pltpu.VMEM((ROWS, D), BF),
            pltpu.VMEM((ROWS, ROWS), BF),
            pltpu.VMEM((ROWS, D), BF),
            pltpu.VMEM((ROWS, ROWS), BF),
            pltpu.VMEM((PAGES, PER, D), BF),
            pltpu.VMEM((PAGES, PER, D), BF),
            pltpu.VMEM((ROWS, D), BF),
            pltpu.VMEM((ROWS, D), BF),
            pltpu.VMEM((ROWS, FF), BF),
            pltpu.VMEM((PAGES, PER, D), BF),
        ]
        + [dma] * 14
        + [dma((16,)), dma((16,)), dma((8,)), dma((8,)), dma((3,))],
        compiler_params=pltpu.CompilerParams(
            collective_id=0, has_side_effects=True, vmem_limit_bytes=48 * 1024 * 1024
        ),
    )(
        page_lengths, occupancy, tile_tokens[0], block_mix, stride_mix,
        jnp.swapaxes(w_gate_up, 1, 2), w_down.T,
    )
    return packed.reshape(1, ROWS, D)


def solution(mesh):
    return jax.shard_map(
        per_device,
        mesh=mesh,
        in_specs=(
            P("page", "tok", None),
            P("page"),
            P("page", "tok"),
            P("tok", None, None),
            P("tok", None, None),
            P(None, None, ("page", "tok")),
            P(None, ("page", "tok")),
        ),
        out_specs=P("tok", "page", None),
        check_vma=False,
    )
```

time: 486 us -> 119 us (0.24)
  the two profiles are of different devices: /device:TPU:224 before, /device:TPU:1 now
where the time goes in v1:
time: 119 us
  Pallas kernels  112 us (94%)
  local copies, waits for them, and re-layouts  6.13 us (5%)
    pallas_call x1, Pallas kernels, per_device(): pl.pallas_call(body, out_shape=jax.ShapeDtypeStruct((PAGES, PER, D), BF),...  112 us
    unnamed x13, local copies, waits for them, and re-layouts  6.13 us

profile of v1, /device:TPU:1, one launch (start us, length us, event | category | flops | bytes accessed | tf_op | source)
XLA Modules:
  0.0 118.9 jit_solution(1228921255896206482)
XLA Ops:
  0.7 0.0 copy-start.5
  0.7 0.6 copy-done.5
  1.3 0.0 copy-start
  1.3 1.2 %copy-done = bf16[1,512,1024]{2,1,0:T(8,128)(2,1)S(1)} copy-done((bf16[1,512,1024]{2,1,0:T(8,128)(2,1)S(1)}, bf16[1,512,1024]{2,1,0:T(8,128)(2,1)}, u32[]{:S(2)}) %copy-start) | copy-done | bytes 1048600
  2.5 0.0 copy-start.1
  2.5 0.9 copy-done.1
  3.4 0.0 copy-start.2
  3.4 0.9 copy-done.2
  4.3 0.0 copy-start.3
  4.3 0.8 copy-done.3
  5.1 0.0 copy-start.4
  5.1 0.7 copy-done.4
  5.8 112.1 %shard_map.73 = bf16[32,16,1024]{2,1,0:T(8,128)(2,1)S(1)} custom-call(s32[1]{0:T(128)S(6)} %copy.9.len_ref, s32[1,4]{1,0:T(1,128)S(1)} %copy-done.5, bf16[512,1024]{1,0:T(8,128)(2,1)S(1)} %bitcast.5, bf16[4,128,128]{2,1,0:T(8,128)(2,1)S(1)} %copy-done.1, bf16[16,32,32]{2,1,0:T(8,128)(2,1)S(1)} %copy-done.2, bf16[2,8,1024]{2,1,0:T(8,128)(2,1)S(1)} %bitcast.6, ...), custom_call_target="tpu_custom_call" | custom-call | tf_op jit(solution)/shard_map/pallas_call | solution.py:299
  117.9 1.0 copy.10
Async XLA Ops:
  0.7 0.7 copy-start.5
  1.3 1.2 %copy-start = (bf16[1,512,1024]{2,1,0:T(8,128)(2,1)S(1)}, bf16[1,512,1024]{2,1,0:T(8,128)(2,1)}, u32[]{:S(2)}) copy-start(bf16[1,512,1024]{2,1,0:T(8,128)(2,1)} %param.7) | copy-start | bytes 3145732
  2.5 0.9 copy-start.1
  3.4 0.9 copy-start.2
  4.3 0.8 copy-start.3
  5.1 0.7 copy-start.4

commit v2 on v1

v2 whole, which is shorter than its diff:
```python
import jax
import jax.numpy as jnp
from jax import lax
from jax.experimental import pallas as pl
from jax.experimental.pallas import tpu as pltpu
from jax.sharding import PartitionSpec as P

NX, NZ, NY, NC = 4, 8, 4, 2
PAGES, TOKS = 32, 8
ROWS, D, FF = 512, 1024, 2048
BLK, NB, PER = 128, 32, 16
EPS = 1e-05
SPLIT = 5
HALF = D // 2
MESH = pl.DeviceIdType.MESH
NT = (((1,), (1,)), ((), ()))
BF, F32 = jnp.bfloat16, jnp.float32


def mod(a, n):
    return lax.rem(a, jnp.int32(n))


def div(a, n):
    return lax.div(a, jnp.int32(n))


def iota(shape, dim):
    return lax.broadcasted_iota(jnp.int32, shape, dim)


def matmul(a, b):
    return jnp.dot(a, b, preferred_element_type=F32)


def matmul_nt(a, b):
    return lax.dot_general(a, b, NT, preferred_element_type=F32)


def rms_round(values):
    scale = lax.rsqrt(jnp.mean(values * values, axis=-1, keepdims=True) + EPS)
    return (values * scale).astype(BF)


def body(
    len_ref, occ_ref, x_hbm, bm_hbm, sm_hbm, wg_hbm, wd_hbm, o_ref,
    x_ref, bm_ref, sm_ref, wg_ref, wd_ref,
    lens_rx, gu_tx, gu_rx, wd_tx, wd_rx, zunit_gu, zunit_wd, gu_lo, gu_hi, wd_lo, wd_hi, fsend, frecv, xm, spread, pre, psel,
    p1tx, p1rx, ynorm, hid, p2tx, p2rx,
    lens_s, lens_r, gu_s, gu_r, wd_s, wd_r, z_s, z_r, tok_s, tok_r,
    p1_s, p1_r, p2_s, p2_r, ring_s, ring_r, core_s, core_r, own_s, in_s, keep_s,
):
    page, tok = lax.axis_index("page"), lax.axis_index("tok")
    x, z = div(page, NZ), mod(page, NZ)
    y, c = div(tok, NC), mod(tok, NC)
    yh, yl = div(y, 2), mod(y, 2)
    sibling = tok + 1 - 2 * c

    def rcopy(src, dst, ssem, rsem, to_page, to_tok):
        return pltpu.make_async_remote_copy(
            src_ref=src, dst_ref=dst, send_sem=ssem, recv_sem=rsem,
            device_id=(to_page, to_tok), device_id_type=MESH,
        )

    def wait_recv(ref, sem):
        rcopy(ref, ref, sem, sem, page, sibling).wait_recv()

    def wait_send(ref, sem):
        rcopy(ref, ref, sem, sem, page, sibling).wait_send()

    loads = [
        pltpu.make_async_copy(src, dst, in_s.at[i])
        for i, (src, dst) in enumerate(
            [(wg_hbm, wg_ref), (wd_hbm, wd_ref), (x_hbm, x_ref), (bm_hbm, bm_ref), (sm_hbm, sm_ref)]
        )
    ]
    for load in loads:
        load.start()
    barrier = pltpu.get_barrier_semaphore()

    @pl.loop(1, PAGES)
    def _(k):
        pl.semaphore_signal(barrier, inc=1, device_id=(mod(page + k, PAGES), tok), device_id_type=MESH)

    @pl.loop(1, TOKS)
    def _(k):
        pl.semaphore_signal(barrier, inc=1, device_id=(page, mod(tok + k, TOKS)), device_id_type=MESH)

    length = len_ref[0]
    loads[0].wait()
    loads[1].wait()
    place8 = (iota((16, 8), 0) == iota((16, 8), 1) + 8 * c).astype(BF)
    place4 = (iota((16, 4), 0) == iota((16, 4), 1) + 4 * mod(tok, 4)).astype(BF)
    for g in range(2):
        gu_tx[g] = matmul(place8, wg_ref[g]).astype(BF)
    wd_all = matmul(place4, wd_ref[...]).astype(BF)
    for q in range(4):
        wd_tx[q] = wd_all[:, q * 512 : (q + 1) * 512]
    lens_rx[page] = jnp.full((8, 128), length, jnp.int32)

    pl.semaphore_wait(barrier, PAGES - 1 + TOKS - 1)

    rcopy(gu_tx.at[1 - c], gu_rx, gu_s, gu_r, page, sibling).start()
    half = 4 * div(tok, 4)
    for k in range(1, 4):
        q = mod(tok + k, 4)
        rcopy(wd_tx.at[q], wd_rx.at[3 - k], wd_s, wd_r, page, half + q).start()

    loads[2].wait()
    loads[3].wait()
    for b in range(4):
        limit = length * occ_ref[0, b] - tok * ROWS - b * BLK
        rows = slice(b * BLK, (b + 1) * BLK)
        live = iota((BLK, D), 0) < limit
        masked = jnp.where(live, x_ref[rows, :].astype(F32), 0.0)
        xm[rows, :] = masked.astype(BF)
        first = matmul(bm_ref[b], rms_round(masked)).astype(BF)
        for h in range(2):
            fsend[h, :, b] = first[:, h * HALF : (h + 1) * HALF].reshape(TOKS, PER, HALF)

    own = []
    for h in range(2):
        own.append(pltpu.make_async_copy(fsend.at[h, tok], frecv.at[h, tok], own_s.at[h]))
        own[h].start()

        @pl.loop(1, TOKS)
        def _(k):
            to = mod(tok + k, TOKS)
            rcopy(fsend.at[h, to], frecv.at[h, tok], tok_s.at[h], tok_r.at[h], page, to).start()

    wait_recv(gu_rx, gu_r)
    wait_recv(wd_rx, wd_r)
    zunit_gu[z] = gu_tx[c] + gu_rx[...]
    zunit_wd[z] = wd_tx[mod(tok, 4)] + wd_rx[0] + wd_rx[1] + wd_rx[2]

    @pl.loop(1, NZ)
    def _(k):
        to = x * NZ + mod(z + k, NZ)
        rcopy(zunit_gu.at[z], zunit_gu.at[z], z_s.at[0], z_r.at[0], to, tok).start()
        rcopy(zunit_wd.at[z], zunit_wd.at[z], z_s.at[1], z_r.at[1], to, tok).start()

    @pl.loop(1, PAGES)
    def _(k):
        rcopy(lens_rx.at[page], lens_rx.at[page], lens_s, lens_r, mod(page + k, PAGES), tok).start()

    loads[4].wait()
    expand = (iota((NB, ROWS), 0) == iota((NB, ROWS), 1) >> 4).astype(BF)
    wide = matmul(sm_ref[...].reshape(ROWS, NB), expand)
    same = (iota((ROWS, ROWS), 1) & 15) == (iota((ROWS, ROWS), 0) >> 5)
    spread[...] = jnp.where(same, wide, 0.0).astype(BF)

    wait_recv(lens_rx.at[pl.ds(0, PAGES - 1)], lens_r)
    lens = lens_rx[:, 0, :]
    lens = jnp.concatenate([lens] * 4, axis=1)
    kept = jnp.clip(lens - tok * ROWS, 0, ROWS)
    who = iota((PAGES, ROWS), 0)
    lane_page = iota((PAGES, ROWS), 1) >> 4
    shift = jnp.sum(jnp.where(who < page, kept, 0), axis=0, keepdims=True)
    start_of = jnp.sum(jnp.where(who < lane_page, kept, 0), axis=0, keepdims=True)
    stop_of = start_of + jnp.sum(jnp.where(who == lane_page, kept, 0), axis=0, keepdims=True)

    @pl.loop(0, 4)
    def _(r):
        rows = pl.ds(pl.multiple_of(r * 128, 128), 128)
        slot = iota((128, ROWS), 0) + r * 128
        turn = (((iota((128, ROWS), 1) + shift) & (ROWS - 1)) == slot).astype(BF)
        pre[rows, :] = matmul(turn, xm[...]).astype(BF)
        psel[rows, :] = matmul(turn, spread[...]).astype(BF)

    los, his, zunits = [gu_lo, wd_lo], [gu_hi, wd_hi], [zunit_gu, zunit_wd]
    mid = (NZ - SPLIT + 1) // 2

    def xlo(xx, cut, kind):
        zs = [pl.ds(0, SPLIT), pl.ds(0, SPLIT // 2), pl.ds(SPLIT // 2, SPLIT - SPLIT // 2)][cut]
        return los[kind].at[c, yh, yl, xx, zs]

    def yhi(yy, cut, kind):
        zs = [pl.ds(0, NZ - SPLIT), pl.ds(0, mid), pl.ds(mid, NZ - SPLIT - mid)][cut]
        return his[kind].at[c, x, div(yy, 2), mod(yy, 2), zs]

    def ylo(yy, cut, kind):
        xs = [pl.ds(0, 4), pl.ds(0, 2), pl.ds(2, 2)][cut]
        return los[kind].at[c, div(yy, 2), mod(yy, 2), xs]

    def xhi(xx, cut, kind):
        ys = [pl.ds(0, 2), pl.ds(0, 1), pl.ds(1, 1)][cut]
        return his[kind].at[c, xx, ys]

    def xdev(by):
        return mod(x + by, NX) * NZ + z, tok

    def ydev(by):
        return page, mod(y + by, NY) * NC + c

    rings = [[(xlo, x, xdev), (yhi, y, ydev)], [(ylo, y, ydev), (xhi, x, xdev)]]

    def ring_copy(stage, kind, hop, which, way):
        piece, me, dev = rings[stage][which]
        by = 1 if way == 0 else 3
        ref = piece(me, 0, kind) if hop == 0 else piece(mod(me + 4 - by, 4), 1 + way, kind)
        src = ref
        if stage == 0 and hop == 0:
            src = zunits[kind].at[pl.ds(0, SPLIT) if which == 0 else pl.ds(SPLIT, NZ - SPLIT)]
        i = stage * 16 + kind * 8 + hop * 4 + which * 2 + way
        return rcopy(src, ref, ring_s.at[i], ring_r.at[i], *dev(by))

    def arriving(stage, kind, hop, which, way):
        piece, me, dev = rings[stage][which]
        by = 1 if way == 0 else 3
        return piece(mod(me + 4 - by, 4), 0, kind) if hop == 0 else piece(mod(me + 2, 4), 1 + way, kind)

    def ring_arrived(stage, kind, hop, which, way):
        i = stage * 16 + kind * 8 + hop * 4 + which * 2 + way
        wait_recv(arriving(stage, kind, hop, which, way), ring_r.at[i])

    both = [(which, way) for which in range(2) for way in range(2)]

    def core_copy(i, ref):
        copy = rcopy(ref, ref, core_s.at[i], core_r.at[i], page, sibling)
        copy.start()
        return copy

    for h in range(2):
        own[h].wait()
        wait_recv(frecv.at[h, pl.ds(0, TOKS - 1)], tok_r.at[h])

        @pl.loop(0, 4)
        def _(r):
            rows = pl.ds(pl.multiple_of(r * 128, 128), 128)
            second = matmul(psel[rows, :], frecv[h].reshape(ROWS, HALF))
            mixed = (pre[rows, h * HALF : (h + 1) * HALF].astype(F32) + second).astype(BF)
            p1tx[h, pl.ds(r * 8, 8)] = mixed.reshape(8, PER, HALF)

        @pl.loop(1, PAGES)
        def _(k):
            to = mod(page + k, PAGES)
            rcopy(p1tx.at[h, to], p1rx.at[h, page], p1_s.at[h], p1_r.at[h], to, tok).start()

        own.append(pltpu.make_async_copy(p1tx.at[h, page], p1rx.at[h, page], own_s.at[2 + h]))
        own[2 + h].start()

    keeps = []
    for kind in range(2):
        wait_recv(zunits[kind].at[pl.ds(0, NZ - 1)], z_r.at[kind])
        for which, way in both:
            ring_copy(0, kind, 0, which, way).start()
        for which in range(2):
            piece, me, dev = rings[0][which]
            span = pl.ds(0, SPLIT) if which == 0 else pl.ds(SPLIT, NZ - SPLIT)
            copy = pltpu.make_async_copy(zunits[kind].at[span], piece(me, 0, kind), keep_s.at[kind * 2 + which])
            copy.start()
            keeps.append(copy)
    for kind in range(2):
        for which, way in both:
            ring_arrived(0, kind, 0, which, way)
            ring_copy(0, kind, 1, which, way).start()
    for copy in keeps:
        copy.wait()
    cores = [[], []]
    for kind in range(2):
        for which, way in both:
            ring_arrived(0, kind, 1, which, way)
        for which, way in both:
            ring_copy(1, kind, 0, which, way).start()
    for kind in range(2):
        for which in range(2):
            piece, me, dev = rings[1][which]
            cores[kind].append(core_copy(kind * 10 + which, piece(me, 0, kind)))

    for h in range(2):
        own[2 + h].wait()
        wait_recv(p1rx.at[h, pl.ds(0, PAGES - 1)], p1_r.at[h])

        @pl.loop(0, 4)
        def _(r):
            row = iota((128, ROWS), 0) + r * 128
            col = iota((128, ROWS), 1)
            target = (row >> 4) * ROWS + page * PER + (row & 15)
            pick = ((row & 15) == (col & 15)) & (target >= start_of) & (target < stop_of)
            mixed = matmul(pick.astype(BF), p1rx[h].reshape(ROWS, HALF))
            p2tx[h, pl.ds(r * 8, 8)] = mixed.astype(BF).reshape(8, PER, HALF)

        @pl.loop(1, PAGES)
        def _(k):
            to = mod(page + k, PAGES)
            rcopy(p2tx.at[h, to], p2rx.at[h, page], p2_s.at[h], p2_r.at[h], to, tok).start()

        own.append(pltpu.make_async_copy(p2tx.at[h, page], p2rx.at[h, page], own_s.at[4 + h]))
        own[4 + h].start()
        for which, way in both:
            ring_arrived(1, h, 0, which, way)
            ring_copy(1, h, 1, which, way).start()
            cores[h].append(core_copy(h * 10 + 2 + which * 2 + way, arriving(1, h, 0, which, way)))

    def last_hop(kind):
        for which, way in both:
            ring_arrived(1, kind, 1, which, way)
            cores[kind].append(core_copy(kind * 10 + 6 + which * 2 + way, arriving(1, kind, 1, which, way)))

    last_hop(0)

    for h in range(2):
        own[4 + h].wait()
        wait_recv(p2rx.at[h, pl.ds(0, PAGES - 1)], p2_r.at[h])

    @pl.loop(0, 4)
    def _(r):
        rows = pl.ds(pl.multiple_of(r * 128, 128), 128)
        mixed = [p2rx[h, pl.ds(r * 8, 8)].reshape(128, HALF).astype(F32) for h in range(2)]
        total = sum(jnp.sum(v * v, axis=-1, keepdims=True) for v in mixed)
        scale = lax.rsqrt(total / D + EPS)
        for h in range(2):
            ynorm[rows, h * HALF : (h + 1) * HALF] = (mixed[h] * scale).astype(BF)

    for copy in cores[0]:
        copy.wait_recv()

    def unit(kind, core, xx, zz, ys):
        if zz < SPLIT:
            return los[kind][core, :, ys, xx, zz]
        return his[kind][core, xx, :, ys, zz - SPLIT]

    @pl.loop(0, 4)
    def _(xx):
        for t in range(2):
            zs = range(4 * t, 4 * t + 4)
            rows = [
                jnp.concatenate([unit(0, core, xx, zz, slice(None)).reshape(64, D) for zz in zs], axis=0)
                for core in range(2)
            ]
            gate, up = matmul_nt(ynorm[...], rows[0]), matmul_nt(ynorm[...], rows[1])
            cols = pl.ds(pl.multiple_of(xx * 512 + t * 256, 256), 256)
            hid[:, cols] = (gate / (1.0 + jnp.exp(-gate)) * up).astype(BF)

    last_hop(1)
    for copy in cores[1]:
        copy.wait_recv()

    @pl.loop(0, 4)
    def _(t):
        half_cols = pl.ds(pl.multiple_of((t & 1) * 256, 256), 256)
        total = p2rx[t >> 1, :, :, half_cols].reshape(ROWS, 256).astype(F32)
        for q in range(4):
            down = jnp.concatenate([unit(1, q % 2, t, zz, q // 2).reshape(32, 512) for zz in range(NZ)], axis=0)
            total = total + matmul_nt(hid[:, q * 512 : (q + 1) * 512], down)
        o_ref[:, pl.ds(pl.multiple_of(t * 256, 256), 256)] = total.astype(BF)

    wait_send(gu_rx, gu_s)
    wait_send(wd_rx, wd_s)
    wait_send(lens_rx.at[pl.ds(0, PAGES - 1)], lens_s)
    for kind in range(2):
        wait_send(zunits[kind].at[pl.ds(0, NZ - 1)], z_s.at[kind])
    for h in range(2):
        wait_send(frecv.at[h, pl.ds(0, TOKS - 1)], tok_s.at[h])
        wait_send(p1tx.at[h, pl.ds(0, PAGES - 1)], p1_s.at[h])
        wait_send(p2tx.at[h, pl.ds(0, PAGES - 1)], p2_s.at[h])
    for stage in range(2):
        for kind in range(2):
            for hop in range(2):
                for which, way in both:
                    ring_copy(stage, kind, hop, which, way).wait_send()
    for copy in cores[0] + cores[1]:
        copy.wait_send()


def per_device(tile_tokens, page_lengths, occupancy, block_mix, stride_mix, w_gate_up, w_down):
    vmem = pl.BlockSpec(memory_space=pltpu.VMEM)
    smem = pl.BlockSpec(memory_space=pltpu.SMEM)
    dma = pltpu.SemaphoreType.DMA
    anywhere = pl.BlockSpec(memory_space=pltpu.HBM)
    packed = pl.pallas_call(
        body,
        out_shape=jax.ShapeDtypeStruct((ROWS, D), BF),
        in_specs=[smem, smem] + [anywhere] * 5,
        out_specs=vmem,
        scratch_shapes=[
            pltpu.VMEM((ROWS, D), BF),
            pltpu.VMEM((4, BLK, BLK), BF),
            pltpu.VMEM((PER, NB, NB), BF),
            pltpu.VMEM((2, 8, D), BF),
            pltpu.VMEM((4, FF), BF),
            pltpu.VMEM((PAGES, 8, 128), jnp.int32),
            pltpu.VMEM((2, 16, D), BF),
            pltpu.VMEM((16, D), BF),
            pltpu.VMEM((4, 16, 512), BF),
            pltpu.VMEM((3, 16, 512), BF),
            pltpu.VMEM((NZ, 16, D), BF),
            pltpu.VMEM((NZ, 16, 512), BF),
            pltpu.VMEM((NC, 2, 2, NX, SPLIT, 16, D), BF),
            pltpu.VMEM((NC, NX, 2, 2, NZ - SPLIT, 16, D), BF),
            pltpu.VMEM((NC, 2, 2, NX, SPLIT, 16, 512), BF),
            pltpu.VMEM((NC, NX, 2, 2, NZ - SPLIT, 16, 512), BF),
            pltpu.VMEM((2, TOKS, 4, PER, HALF), BF),
            pltpu.VMEM((2, TOKS, 4, PER, HALF), BF),
            pltpu.VMEM((ROWS, D), BF),
            pltpu.VMEM((ROWS, ROWS), BF),
            pltpu.VMEM((ROWS, D), BF),
            pltpu.VMEM((ROWS, ROWS), BF),
            pltpu.VMEM((2, PAGES, PER, HALF), BF),
            pltpu.VMEM((2, PAGES, PER, HALF), BF),
            pltpu.VMEM((ROWS, D), BF),
            pltpu.VMEM((ROWS, FF), BF),
            pltpu.VMEM((2, PAGES, PER, HALF), BF),
            pltpu.VMEM((2, PAGES, PER, HALF), BF),
        ]
        + [dma] * 6
        + [dma((2,))] * 8
        + [dma((32,)), dma((32,)), dma((20,)), dma((20,)), dma((6,)), dma((5,)), dma((4,))],
        compiler_params=pltpu.CompilerParams(
            collective_id=0, has_side_effects=True, vmem_limit_bytes=62 * 1024 * 1024
        ),
    )(
        page_lengths, occupancy, tile_tokens[0], block_mix, stride_mix,
        jnp.swapaxes(w_gate_up, 1, 2), w_down.T,
    )
    return packed.reshape(1, ROWS, D)


def solution(mesh):
    return jax.shard_map(
        per_device,
        mesh=mesh,
        in_specs=(
            P("page", "tok", None),
            P("page"),
            P("page", "tok"),
            P("tok", None, None),
            P("tok", None, None),
            P(None, None, ("page", "tok")),
            P(None, ("page", "tok")),
        ),
        out_specs=P("tok", "page", None),
        check_vma=False,
    )
```

time: 119 us -> 99.3 us (0.83)
  Pallas kernels: 112 us -> 96.2 us
  local copies, waits for them, and re-layouts: 6.13 us -> 2.26 us
    pallas_call x1, Pallas kernels: 112 us -> 96.2 us  [per_device(): pl.pallas_call(body, out_shape=jax.ShapeDtypeStruct((ROWS, D), BF), in_sp...]
    unnamed x13 -> x1, local copies, waits for them, and re-layouts: 6.13 us -> 2.26 us
where the time goes in v2:
time: 99.3 us; the launch traced here: 99.2 us
  Pallas kernels  96.2 us (97%)
  local copies, waits for them, and re-layouts  2.26 us (2%)
    pallas_call x1, Pallas kernels, per_device(): pl.pallas_call(body, out_shape=jax.ShapeDtypeStruct((ROWS, D), BF), in_sp...  96.2 us
    unnamed x1, local copies, waits for them, and re-layouts  2.26 us

profile of v2, /device:TPU:1, one launch (start us, length us, event | category | flops | bytes accessed | tf_op | source)
XLA Modules:
  0.0 99.2 jit_solution(17021274935080970381)
XLA Ops:
  0.7 96.2 %shard_map.73 = bf16[512,1024]{1,0:T(8,128)(2,1)} custom-call(s32[1]{0:T(128)S(6)} %copy.9.len_ref, s32[1,4]{1,0:T(1,128)} %occ_ref.1, bf16[512,1024]{1,0:T(8,128)(2,1)} %bitcast.5, bf16[4,128,128]{2,1,0:T(8,128)(2,1)} %bm_hbm.1, bf16[16,32,32]{2,1,0:T(8,128)(2,1)} %sm_hbm.1, bf16[2,8,1024]{2,1,0:T(8,128)(2,1)} %bitcast.6, bf16[4,2048]{1,0:T(4,128)(2,1)} %bitcast.7), custom_call_target="tpu_custom_call" | custom-call | tf_op jit(solution)/shard_map/pallas_call | solution.py:371
  96.9 2.3 %copy.10 = bf16[1,512,1024]{2,1,0:T(8,128)(2,1)} copy(bf16[1,512,1024]{2,1,0:T(8,128)(2,1)} %bitcast.4) | data formatting | bytes 2097152

commit v3 on v2

--- a/solution.py
+++ b/solution.py
@@ -96,15 +96,7 @@
     wd_all = matmul(place4, wd_ref[...]).astype(BF)
     for q in range(4):
         wd_tx[q] = wd_all[:, q * 512 : (q + 1) * 512]
-    lens_rx[page] = jnp.full((8, 128), length, jnp.int32)
-
-    pl.semaphore_wait(barrier, PAGES - 1 + TOKS - 1)
-
-    rcopy(gu_tx.at[1 - c], gu_rx, gu_s, gu_r, page, sibling).start()
-    half = 4 * div(tok, 4)
-    for k in range(1, 4):
-        q = mod(tok + k, 4)
-        rcopy(wd_tx.at[q], wd_rx.at[3 - k], wd_s, wd_r, page, half + q).start()
+    lens_rx[page] = jnp.full((1, 128), length, jnp.int32)
 
     loads[2].wait()
     loads[3].wait()
@@ -118,8 +110,17 @@
         for h in range(2):
             fsend[h, :, b] = first[:, h * HALF : (h + 1) * HALF].reshape(TOKS, PER, HALF)
 
+    pl.semaphore_wait(barrier, PAGES - 1 + TOKS - 1)
+
+    rcopy(gu_tx.at[1 - c], gu_rx, gu_s, gu_r, page, sibling).start()
+    half = 4 * div(tok, 4)
+    for k in range(1, 4):
+        q = mod(tok + k, 4)
+        rcopy(wd_tx.at[q], wd_rx.at[3 - k], wd_s, wd_r, page, half + q).start()
+
     own = []
-    for h in range(2):
+
+    def send_first(h):
         own.append(pltpu.make_async_copy(fsend.at[h, tok], frecv.at[h, tok], own_s.at[h]))
         own[h].start()
 
@@ -127,6 +128,14 @@
         def _(k):
             to = mod(tok + k, TOKS)
             rcopy(fsend.at[h, to], frecv.at[h, tok], tok_s.at[h], tok_r.at[h], page, to).start()
+
+    send_first(0)
+
+    @pl.loop(1, PAGES)
+    def _(k):
+        rcopy(lens_rx.at[page], lens_rx.at[page], lens_s, lens_r, mod(page + k, PAGES), tok).start()
+
+    send_first(1)
 
     wait_recv(gu_rx, gu_r)
     wait_recv(wd_rx, wd_r)
@@ -138,10 +147,6 @@
         to = x * NZ + mod(z + k, NZ)
         rcopy(zunit_gu.at[z], zunit_gu.at[z], z_s.at[0], z_r.at[0], to, tok).start()
         rcopy(zunit_wd.at[z], zunit_wd.at[z], z_s.at[1], z_r.at[1], to, tok).start()
-
-    @pl.loop(1, PAGES)
-    def _(k):
-        rcopy(lens_rx.at[page], lens_rx.at[page], lens_s, lens_r, mod(page + k, PAGES), tok).start()
 
     loads[4].wait()
     expand = (iota((NB, ROWS), 0) == iota((NB, ROWS), 1) >> 4).astype(BF)
@@ -379,7 +384,7 @@
             pltpu.VMEM((PER, NB, NB), BF),
             pltpu.VMEM((2, 8, D), BF),
             pltpu.VMEM((4, FF), BF),
-            pltpu.VMEM((PAGES, 8, 128), jnp.int32),
+            pltpu.VMEM((PAGES, 1, 128), jnp.int32),
             pltpu.VMEM((2, 16, D), BF),
             pltpu.VMEM((16, D), BF),
             pltpu.VMEM((4, 16, 512), BF),
@@ -407,11 +412,14 @@
         + [dma((2,))] * 8
         + [dma((32,)), dma((32,)), dma((20,)), dma((20,)), dma((6,)), dma((5,)), dma((4,))],
         compiler_params=pltpu.CompilerParams(
-            collective_id=0, has_side_effects=True, vmem_limit_bytes=62 * 1024 * 1024
+            collective_id=0, has_side_effects=True, vmem_limit_bytes=48 * 1024 * 1024
         ),
     )(
-        page_lengths, occupancy, tile_tokens[0], block_mix, stride_mix,
-        jnp.swapaxes(w_gate_up, 1, 2), w_down.T,
+        page_lengths, occupancy,
+        *(
+            pltpu.with_memory_space_constraint(v, pltpu.HBM)
+            for v in (tile_tokens[0], block_mix, stride_mix, jnp.swapaxes(w_gate_up, 1, 2), w_down.T)
+        ),
     )
     return packed.reshape(1, ROWS, D)
 

time: 99.3 us -> 92.6 us (0.933)
  Pallas kernels: 96.2 us -> 90.2 us
    pallas_call x1, Pallas kernels: 96.2 us -> 90.2 us  [per_device(): pl.pallas_call(body, out_shape=jax.ShapeDtypeStruct((ROWS, D), BF), in_sp...]
    unnamed x1 -> x3, local copies, waits for them, and re-layouts: 2.26 us -> 1.62 us
where the time goes in v3:
time: 92.6 us; the launch traced here: 92.4 us
  Pallas kernels  90.2 us (97%)
  local copies, waits for them, and re-layouts  1.62 us (2%)
    pallas_call x1, Pallas kernels, per_device(): pl.pallas_call(body, out_shape=jax.ShapeDtypeStruct((ROWS, D), BF), in_sp...  90.2 us

profile of v3, /device:TPU:1, one launch (start us, length us, event | category | flops | bytes accessed | tf_op | source)
XLA Modules:
  0.0 92.4 jit_solution(14104128548422006058)
XLA Ops:
  0.7 0.0 copy-start
  0.7 0.6 copy-done
  1.3 90.2 %shard_map.73 = bf16[512,1024]{1,0:T(8,128)(2,1)S(1)} custom-call(s32[1]{0:T(128)S(6)} %copy.9.len_ref, s32[1,4]{1,0:T(1,128)S(1)} %copy-done, bf16[512,1024]{1,0:T(8,128)(2,1)} %bitcast.5, bf16[4,128,128]{2,1,0:T(8,128)(2,1)} %bm_hbm.1, bf16[16,32,32]{2,1,0:T(8,128)(2,1)} %sm_hbm.1, bf16[2,8,1024]{2,1,0:T(8,128)(2,1)} %bitcast.6, bf16[4,2048]{1,0:T(4,128)(2,1)} %bitcast.7), custom_call_target="tpu_custom_call" | custom-call | tf_op jit(solution)/shard_map/pallas_call | solution.py:376
  91.5 1.0 %copy.10 = bf16[1,512,1024]{2,1,0:T(8,128)(2,1)} copy(bf16[1,512,1024]{2,1,0:T(8,128)(2,1)S(1)} %bitcast.4) | data formatting | bytes 2097152
Async XLA Ops:
  0.7 0.7 copy-start

commit v4 on v3

--- a/solution.py
+++ b/solution.py
@@ -11,7 +11,7 @@
 BLK, NB, PER = 128, 32, 16
 EPS = 1e-05
 SPLIT = 5
-HALF = D // 2
+CHUNKS = ((0, 256), (256, 256), (512, 512))
 MESH = pl.DeviceIdType.MESH
 NT = (((1,), (1,)), ((), ()))
 BF, F32 = jnp.bfloat16, jnp.float32
@@ -45,10 +45,11 @@
 def body(
     len_ref, occ_ref, x_hbm, bm_hbm, sm_hbm, wg_hbm, wd_hbm, o_ref,
     x_ref, bm_ref, sm_ref, wg_ref, wd_ref,
-    lens_rx, gu_tx, gu_rx, wd_tx, wd_rx, zunit_gu, zunit_wd, gu_lo, gu_hi, wd_lo, wd_hi, fsend, frecv, xm, spread, pre, psel,
-    p1tx, p1rx, ynorm, hid, p2tx, p2rx,
+    lens_rx, gu_tx, gu_rx, wd_tx, wd_rx, zunit_gu, zunit_wd, gu_lo, gu_hi, wd_lo, wd_hi, xm, spread, pre, psel, picks,
+    ynorm, hid,
+    fsend, frecv, p1tx, p1rx, p2tx, p2rx,
     lens_s, lens_r, gu_s, gu_r, wd_s, wd_r, z_s, z_r, tok_s, tok_r,
-    p1_s, p1_r, p2_s, p2_r, ring_s, ring_r, core_s, core_r, own_s, in_s, keep_s,
+    p1_s, p1_r, p2_s, p2_r, ring_s, ring_r, core_s, core_r, own_s, in_s, keep_s, z2_s, z2_r,
 ):
     page, tok = lax.axis_index("page"), lax.axis_index("tok")
     x, z = div(page, NZ), mod(page, NZ)
@@ -107,10 +108,14 @@
         masked = jnp.where(live, x_ref[rows, :].astype(F32), 0.0)
         xm[rows, :] = masked.astype(BF)
         first = matmul(bm_ref[b], rms_round(masked)).astype(BF)
-        for h in range(2):
-            fsend[h, :, b] = first[:, h * HALF : (h + 1) * HALF].reshape(TOKS, PER, HALF)
+        for h, (at, n) in enumerate(CHUNKS):
+            fsend[h][:, b] = first[:, at : at + n].reshape(TOKS, PER, n)
 
     pl.semaphore_wait(barrier, PAGES - 1 + TOKS - 1)
+
+    @pl.loop(1, PAGES)
+    def _(k):
+        rcopy(lens_rx.at[page], lens_rx.at[page], lens_s, lens_r, mod(page + k, PAGES), tok).start()
 
     rcopy(gu_tx.at[1 - c], gu_rx, gu_s, gu_r, page, sibling).start()
     half = 4 * div(tok, 4)
@@ -119,34 +124,28 @@
         rcopy(wd_tx.at[q], wd_rx.at[3 - k], wd_s, wd_r, page, half + q).start()
 
     own = []
-
-    def send_first(h):
-        own.append(pltpu.make_async_copy(fsend.at[h, tok], frecv.at[h, tok], own_s.at[h]))
+    for h in range(len(CHUNKS)):
+        own.append(pltpu.make_async_copy(fsend[h].at[tok], frecv[h].at[tok], own_s.at[h]))
         own[h].start()
 
         @pl.loop(1, TOKS)
         def _(k):
             to = mod(tok + k, TOKS)
-            rcopy(fsend.at[h, to], frecv.at[h, tok], tok_s.at[h], tok_r.at[h], page, to).start()
-
-    send_first(0)
-
-    @pl.loop(1, PAGES)
-    def _(k):
-        rcopy(lens_rx.at[page], lens_rx.at[page], lens_s, lens_r, mod(page + k, PAGES), tok).start()
-
-    send_first(1)
+            rcopy(fsend[h].at[to], frecv[h].at[tok], tok_s.at[h], tok_r.at[h], page, to).start()
 
     wait_recv(gu_rx, gu_r)
     wait_recv(wd_rx, wd_r)
     zunit_gu[z] = gu_tx[c] + gu_rx[...]
     zunit_wd[z] = wd_tx[mod(tok, 4)] + wd_rx[0] + wd_rx[1] + wd_rx[2]
-
-    @pl.loop(1, NZ)
-    def _(k):
-        to = x * NZ + mod(z + k, NZ)
-        rcopy(zunit_gu.at[z], zunit_gu.at[z], z_s.at[0], z_r.at[0], to, tok).start()
-        rcopy(zunit_wd.at[z], zunit_wd.at[z], z_s.at[1], z_r.at[1], to, tok).start()
+    zunits = [zunit_gu, zunit_wd]
+
+    def z_copy(kind, origin, by, ssem, rsem):
+        ref = zunits[kind].at[mod(z + origin + NZ, NZ)]
+        return rcopy(ref, ref, ssem.at[kind], rsem.at[kind], x * NZ + mod(z + by + NZ, NZ), tok)
+
+    for kind in range(2):
+        for by in (2, -2, 1, -1):
+            z_copy(kind, 0, by, z_s, z_r).start()
 
     loads[4].wait()
     expand = (iota((NB, ROWS), 0) == iota((NB, ROWS), 1) >> 4).astype(BF)
@@ -172,7 +171,7 @@
         pre[rows, :] = matmul(turn, xm[...]).astype(BF)
         psel[rows, :] = matmul(turn, spread[...]).astype(BF)
 
-    los, his, zunits = [gu_lo, wd_lo], [gu_hi, wd_hi], [zunit_gu, zunit_wd]
+    los, his = [gu_lo, wd_lo], [gu_hi, wd_hi]
     mid = (NZ - SPLIT + 1) // 2
 
     def xlo(xx, cut, kind):
@@ -225,28 +224,54 @@
         copy.start()
         return copy
 
-    for h in range(2):
+    def turn_rows(h):
+        at, n = CHUNKS[h]
         own[h].wait()
-        wait_recv(frecv.at[h, pl.ds(0, TOKS - 1)], tok_r.at[h])
+        wait_recv(frecv[h].at[pl.ds(0, TOKS - 1)], tok_r.at[h])
 
         @pl.loop(0, 4)
         def _(r):
             rows = pl.ds(pl.multiple_of(r * 128, 128), 128)
-            second = matmul(psel[rows, :], frecv[h].reshape(ROWS, HALF))
-            mixed = (pre[rows, h * HALF : (h + 1) * HALF].astype(F32) + second).astype(BF)
-            p1tx[h, pl.ds(r * 8, 8)] = mixed.reshape(8, PER, HALF)
+            second = matmul(psel[rows, :], frecv[h][...].reshape(ROWS, n))
+            mixed = (pre[rows, at : at + n].astype(F32) + second).astype(BF)
+            p1tx[h][pl.ds(r * 8, 8)] = mixed.reshape(8, PER, n)
 
         @pl.loop(1, PAGES)
         def _(k):
             to = mod(page + k, PAGES)
-            rcopy(p1tx.at[h, to], p1rx.at[h, page], p1_s.at[h], p1_r.at[h], to, tok).start()
-
-        own.append(pltpu.make_async_copy(p1tx.at[h, page], p1rx.at[h, page], own_s.at[2 + h]))
-        own[2 + h].start()
-
-    keeps = []
-    for kind in range(2):
-        wait_recv(zunits[kind].at[pl.ds(0, NZ - 1)], z_r.at[kind])
+            rcopy(p1tx[h].at[to], p1rx[h].at[page], p1_s.at[h], p1_r.at[h], to, tok).start()
+
+        own1.append(pltpu.make_async_copy(p1tx[h].at[page], p1rx[h].at[page], own_s.at[3 + h]))
+        own1[h].start()
+
+    def pack_rows(h):
+        n = CHUNKS[h][1]
+        own1[h].wait()
+        wait_recv(p1rx[h].at[pl.ds(0, PAGES - 1)], p1_r.at[h])
+
+        @pl.loop(0, 4)
+        def _(r):
+            rows = pl.ds(pl.multiple_of(r * 128, 128), 128)
+            mixed = matmul(picks[rows, :], p1rx[h][...].reshape(ROWS, n))
+            p2tx[h][pl.ds(r * 8, 8)] = mixed.astype(BF).reshape(8, PER, n)
+
+        @pl.loop(1, PAGES)
+        def _(k):
+            to = mod(page + k, PAGES)
+            rcopy(p2tx[h].at[to], p2rx[h].at[page], p2_s.at[h], p2_r.at[h], to, tok).start()
+
+        own2.append(pltpu.make_async_copy(p2tx[h].at[page], p2rx[h].at[page], own_s.at[6 + h]))
+        own2[h].start()
+
+    own1, own2, keeps, cores = [], [], [], [[], []]
+    for kind in range(2):
+        wait_recv(zunits[kind].at[pl.ds(0, 4)], z_r.at[kind])
+        z_copy(kind, -2, 1, z2_s, z2_r).start()
+        z_copy(kind, 2, -1, z2_s, z2_r).start()
+        z_copy(kind, 4 * kind - 2, 2 - 4 * kind, z2_s, z2_r).start()
+    turn_rows(0)
+    for kind in range(2):
+        wait_recv(zunits[kind].at[pl.ds(0, 3)], z2_r.at[kind])
         for which, way in both:
             ring_copy(0, kind, 0, which, way).start()
         for which in range(2):
@@ -255,47 +280,41 @@
             copy = pltpu.make_async_copy(zunits[kind].at[span], piece(me, 0, kind), keep_s.at[kind * 2 + which])
             copy.start()
             keeps.append(copy)
+    turn_rows(1)
     for kind in range(2):
         for which, way in both:
             ring_arrived(0, kind, 0, which, way)
             ring_copy(0, kind, 1, which, way).start()
     for copy in keeps:
         copy.wait()
-    cores = [[], []]
+    turn_rows(2)
+
+    @pl.loop(0, 4)
+    def _(r):
+        row = iota((128, ROWS), 0) + r * 128
+        col = iota((128, ROWS), 1)
+        target = (row >> 4) * ROWS + page * PER + (row & 15)
+        pick = ((row & 15) == (col & 15)) & (target >= start_of) & (target < stop_of)
+        picks[pl.ds(pl.multiple_of(r * 128, 128), 128), :] = pick.astype(BF)
+
     for kind in range(2):
         for which, way in both:
             ring_arrived(0, kind, 1, which, way)
         for which, way in both:
             ring_copy(1, kind, 0, which, way).start()
+    pack_rows(0)
     for kind in range(2):
         for which in range(2):
             piece, me, dev = rings[1][which]
             cores[kind].append(core_copy(kind * 10 + which, piece(me, 0, kind)))
-
-    for h in range(2):
-        own[2 + h].wait()
-        wait_recv(p1rx.at[h, pl.ds(0, PAGES - 1)], p1_r.at[h])
-
-        @pl.loop(0, 4)
-        def _(r):
-            row = iota((128, ROWS), 0) + r * 128
-            col = iota((128, ROWS), 1)
-            target = (row >> 4) * ROWS + page * PER + (row & 15)
-            pick = ((row & 15) == (col & 15)) & (target >= start_of) & (target < stop_of)
-            mixed = matmul(pick.astype(BF), p1rx[h].reshape(ROWS, HALF))
-            p2tx[h, pl.ds(r * 8, 8)] = mixed.astype(BF).reshape(8, PER, HALF)
-
-        @pl.loop(1, PAGES)
-        def _(k):
-            to = mod(page + k, PAGES)
-            rcopy(p2tx.at[h, to], p2rx.at[h, page], p2_s.at[h], p2_r.at[h], to, tok).start()
-
-        own.append(pltpu.make_async_copy(p2tx.at[h, page], p2rx.at[h, page], own_s.at[4 + h]))
-        own[4 + h].start()
-        for which, way in both:
-            ring_arrived(1, h, 0, which, way)
-            ring_copy(1, h, 1, which, way).start()
-            cores[h].append(core_copy(h * 10 + 2 + which * 2 + way, arriving(1, h, 0, which, way)))
+    pack_rows(1)
+    for kind in range(2):
+        for which, way in both:
+            ring_arrived(1, kind, 0, which, way)
+            ring_copy(1, kind, 1, which, way).start()
+            cores[kind].append(core_copy(kind * 10 + 2 + which * 2 + way, arriving(1, kind, 0, which, way)))
+        if kind == 0:
+            pack_rows(2)
 
     def last_hop(kind):
         for which, way in both:
@@ -304,18 +323,18 @@
 
     last_hop(0)
 
-    for h in range(2):
-        own[4 + h].wait()
-        wait_recv(p2rx.at[h, pl.ds(0, PAGES - 1)], p2_r.at[h])
+    for h in range(len(CHUNKS)):
+        own2[h].wait()
+        wait_recv(p2rx[h].at[pl.ds(0, PAGES - 1)], p2_r.at[h])
 
     @pl.loop(0, 4)
     def _(r):
         rows = pl.ds(pl.multiple_of(r * 128, 128), 128)
-        mixed = [p2rx[h, pl.ds(r * 8, 8)].reshape(128, HALF).astype(F32) for h in range(2)]
+        mixed = [p2rx[h][pl.ds(r * 8, 8)].reshape(128, n).astype(F32) for h, (at, n) in enumerate(CHUNKS)]
         total = sum(jnp.sum(v * v, axis=-1, keepdims=True) for v in mixed)
         scale = lax.rsqrt(total / D + EPS)
-        for h in range(2):
-            ynorm[rows, h * HALF : (h + 1) * HALF] = (mixed[h] * scale).astype(BF)
+        for v, (at, n) in zip(mixed, CHUNKS):
+            ynorm[rows, at : at + n] = (v * scale).astype(BF)
 
     for copy in cores[0]:
         copy.wait_recv()
@@ -341,24 +360,24 @@
     for copy in cores[1]:
         copy.wait_recv()
 
-    @pl.loop(0, 4)
-    def _(t):
-        half_cols = pl.ds(pl.multiple_of((t & 1) * 256, 256), 256)
-        total = p2rx[t >> 1, :, :, half_cols].reshape(ROWS, 256).astype(F32)
+    for t, h in enumerate((0, 1, 2, 2)):
+        at = t * 256 - CHUNKS[h][0]
+        total = p2rx[h][:, :, at : at + 256].reshape(ROWS, 256).astype(F32)
         for q in range(4):
             down = jnp.concatenate([unit(1, q % 2, t, zz, q // 2).reshape(32, 512) for zz in range(NZ)], axis=0)
             total = total + matmul_nt(hid[:, q * 512 : (q + 1) * 512], down)
-        o_ref[:, pl.ds(pl.multiple_of(t * 256, 256), 256)] = total.astype(BF)
+        o_ref[:, t * 256 : (t + 1) * 256] = total.astype(BF)
 
     wait_send(gu_rx, gu_s)
     wait_send(wd_rx, wd_s)
     wait_send(lens_rx.at[pl.ds(0, PAGES - 1)], lens_s)
     for kind in range(2):
-        wait_send(zunits[kind].at[pl.ds(0, NZ - 1)], z_s.at[kind])
-    for h in range(2):
-        wait_send(frecv.at[h, pl.ds(0, TOKS - 1)], tok_s.at[h])
-        wait_send(p1tx.at[h, pl.ds(0, PAGES - 1)], p1_s.at[h])
-        wait_send(p2tx.at[h, pl.ds(0, PAGES - 1)], p2_s.at[h])
+        wait_send(zunits[kind].at[pl.ds(0, 4)], z_s.at[kind])
+        wait_send(zunits[kind].at[pl.ds(0, 3)], z2_s.at[kind])
+    for h in range(len(CHUNKS)):
+        wait_send(frecv[h].at[pl.ds(0, TOKS - 1)], tok_s.at[h])
+        wait_send(p1tx[h].at[pl.ds(0, PAGES - 1)], p1_s.at[h])
+        wait_send(p2tx[h].at[pl.ds(0, PAGES - 1)], p2_s.at[h])
     for stage in range(2):
         for kind in range(2):
             for hop in range(2):
@@ -395,22 +414,20 @@
             pltpu.VMEM((NC, NX, 2, 2, NZ - SPLIT, 16, D), BF),
             pltpu.VMEM((NC, 2, 2, NX, SPLIT, 16, 512), BF),
             pltpu.VMEM((NC, NX, 2, 2, NZ - SPLIT, 16, 512), BF),
-            pltpu.VMEM((2, TOKS, 4, PER, HALF), BF),
-            pltpu.VMEM((2, TOKS, 4, PER, HALF), BF),
             pltpu.VMEM((ROWS, D), BF),
             pltpu.VMEM((ROWS, ROWS), BF),
             pltpu.VMEM((ROWS, D), BF),
             pltpu.VMEM((ROWS, ROWS), BF),
-            pltpu.VMEM((2, PAGES, PER, HALF), BF),
-            pltpu.VMEM((2, PAGES, PER, HALF), BF),
+            pltpu.VMEM((ROWS, ROWS), BF),
             pltpu.VMEM((ROWS, D), BF),
             pltpu.VMEM((ROWS, FF), BF),
-            pltpu.VMEM((2, PAGES, PER, HALF), BF),
-            pltpu.VMEM((2, PAGES, PER, HALF), BF),
+            *[[pltpu.VMEM((TOKS, 4, PER, n), BF) for at, n in CHUNKS] for k in range(2)],
+            *[[pltpu.VMEM((PAGES, PER, n), BF) for at, n in CHUNKS] for k in range(4)],
         ]
         + [dma] * 6
-        + [dma((2,))] * 8
-        + [dma((32,)), dma((32,)), dma((20,)), dma((20,)), dma((6,)), dma((5,)), dma((4,))],
+        + [dma((2,))] * 2
+        + [dma((3,))] * 6
+        + [dma((32,)), dma((32,)), dma((20,)), dma((20,)), dma((9,)), dma((5,)), dma((4,)), dma((2,)), dma((2,))],
         compiler_params=pltpu.CompilerParams(
             collective_id=0, has_side_effects=True, vmem_limit_bytes=48 * 1024 * 1024
         ),

time: 92.6 us -> 86.8 us (0.937)
  Pallas kernels: 90.2 us -> 84.4 us
    pallas_call x1, Pallas kernels: 90.2 us -> 84.4 us  [per_device(): pl.pallas_call(body, out_shape=jax.ShapeDtypeStruct((ROWS, D), BF), in_sp...]
where the time goes in v4:
time: 86.8 us; the launch traced here: 86.7 us
  Pallas kernels  84.4 us (97%)
  local copies, waits for them, and re-layouts  1.62 us (2%)
    pallas_call x1, Pallas kernels, per_device(): pl.pallas_call(body, out_shape=jax.ShapeDtypeStruct((ROWS, D), BF), in_sp...  84.4 us

profile of v4, /device:TPU:1, one launch (start us, length us, event | category | flops | bytes accessed | tf_op | source)
XLA Modules:
  0.0 86.7 jit_solution(18309917171755728360)
XLA Ops:
  0.7 0.0 copy-start
  0.7 0.6 copy-done
  1.3 84.4 %shard_map.73 = bf16[512,1024]{1,0:T(8,128)(2,1)S(1)} custom-call(s32[1]{0:T(128)S(6)} %copy.9.len_ref, s32[1,4]{1,0:T(1,128)S(1)} %copy-done, bf16[512,1024]{1,0:T(8,128)(2,1)} %bitcast.5, bf16[4,128,128]{2,1,0:T(8,128)(2,1)} %bm_hbm.1, bf16[16,32,32]{2,1,0:T(8,128)(2,1)} %sm_hbm.1, bf16[2,8,1024]{2,1,0:T(8,128)(2,1)} %bitcast.6, bf16[4,2048]{1,0:T(4,128)(2,1)} %bitcast.7), custom_call_target="tpu_custom_call" | custom-call | tf_op jit(solution)/shard_map/pallas_call | solution.py:395
  85.7 1.0 %copy.10 = bf16[1,512,1024]{2,1,0:T(8,128)(2,1)} copy(bf16[1,512,1024]{2,1,0:T(8,128)(2,1)S(1)} %bitcast.4) | data formatting | bytes 2097152
Async XLA Ops:
  0.7 0.7 copy-start

commit v5 on v4

--- a/solution.py
+++ b/solution.py
@@ -10,7 +10,7 @@
 ROWS, D, FF = 512, 1024, 2048
 BLK, NB, PER = 128, 32, 16
 EPS = 1e-05
-SPLIT = 5
+SPLITS = (5, 6)
 CHUNKS = ((0, 256), (256, 256), (512, 512))
 MESH = pl.DeviceIdType.MESH
 NT = (((1,), (1,)), ((), ()))
@@ -46,7 +46,7 @@
     len_ref, occ_ref, x_hbm, bm_hbm, sm_hbm, wg_hbm, wd_hbm, o_ref,
     x_ref, bm_ref, sm_ref, wg_ref, wd_ref,
     lens_rx, gu_tx, gu_rx, wd_tx, wd_rx, zunit_gu, zunit_wd, gu_lo, gu_hi, wd_lo, wd_hi, xm, spread, pre, psel, picks,
-    ynorm, hid,
+    sums, scales, hid,
     fsend, frecv, p1tx, p1rx, p2tx, p2rx,
     lens_s, lens_r, gu_s, gu_r, wd_s, wd_r, z_s, z_r, tok_s, tok_r,
     p1_s, p1_r, p2_s, p2_r, ring_s, ring_r, core_s, core_r, own_s, in_s, keep_s, z2_s, z2_r,
@@ -113,10 +113,6 @@
 
     pl.semaphore_wait(barrier, PAGES - 1 + TOKS - 1)
 
-    @pl.loop(1, PAGES)
-    def _(k):
-        rcopy(lens_rx.at[page], lens_rx.at[page], lens_s, lens_r, mod(page + k, PAGES), tok).start()
-
     rcopy(gu_tx.at[1 - c], gu_rx, gu_s, gu_r, page, sibling).start()
     half = 4 * div(tok, 4)
     for k in range(1, 4):
@@ -124,7 +120,8 @@
         rcopy(wd_tx.at[q], wd_rx.at[3 - k], wd_s, wd_r, page, half + q).start()
 
     own = []
-    for h in range(len(CHUNKS)):
+
+    def send_first(h):
         own.append(pltpu.make_async_copy(fsend[h].at[tok], frecv[h].at[tok], own_s.at[h]))
         own[h].start()
 
@@ -132,6 +129,12 @@
         def _(k):
             to = mod(tok + k, TOKS)
             rcopy(fsend[h].at[to], frecv[h].at[tok], tok_s.at[h], tok_r.at[h], page, to).start()
+
+    send_first(0)
+
+    @pl.loop(1, PAGES)
+    def _(k):
+        rcopy(lens_rx.at[page], lens_rx.at[page], lens_s, lens_r, mod(page + k, PAGES), tok).start()
 
     wait_recv(gu_rx, gu_r)
     wait_recv(wd_rx, wd_r)
@@ -146,6 +149,8 @@
     for kind in range(2):
         for by in (2, -2, 1, -1):
             z_copy(kind, 0, by, z_s, z_r).start()
+    send_first(1)
+    send_first(2)
 
     loads[4].wait()
     expand = (iota((NB, ROWS), 0) == iota((NB, ROWS), 1) >> 4).astype(BF)
@@ -172,14 +177,16 @@
         psel[rows, :] = matmul(turn, spread[...]).astype(BF)
 
     los, his = [gu_lo, wd_lo], [gu_hi, wd_hi]
-    mid = (NZ - SPLIT + 1) // 2
 
     def xlo(xx, cut, kind):
-        zs = [pl.ds(0, SPLIT), pl.ds(0, SPLIT // 2), pl.ds(SPLIT // 2, SPLIT - SPLIT // 2)][cut]
+        n = SPLITS[kind]
+        zs = [pl.ds(0, n), pl.ds(0, n // 2), pl.ds(n // 2, n - n // 2)][cut]
         return los[kind].at[c, yh, yl, xx, zs]
 
     def yhi(yy, cut, kind):
-        zs = [pl.ds(0, NZ - SPLIT), pl.ds(0, mid), pl.ds(mid, NZ - SPLIT - mid)][cut]
+        n = NZ - SPLITS[kind]
+        mid = (n + 1) // 2
+        zs = [pl.ds(0, n), pl.ds(0, mid), pl.ds(mid, n - mid)][cut]
         return his[kind].at[c, x, div(yy, 2), mod(yy, 2), zs]
 
     def ylo(yy, cut, kind):
@@ -204,7 +211,7 @@
         ref = piece(me, 0, kind) if hop == 0 else piece(mod(me + 4 - by, 4), 1 + way, kind)
         src = ref
         if stage == 0 and hop == 0:
-            src = zunits[kind].at[pl.ds(0, SPLIT) if which == 0 else pl.ds(SPLIT, NZ - SPLIT)]
+            src = zunits[kind].at[pl.ds(0, SPLITS[kind]) if which == 0 else pl.ds(SPLITS[kind], NZ - SPLITS[kind])]
         i = stage * 16 + kind * 8 + hop * 4 + which * 2 + way
         return rcopy(src, ref, ring_s.at[i], ring_r.at[i], *dev(by))
 
@@ -216,6 +223,14 @@
     def ring_arrived(stage, kind, hop, which, way):
         i = stage * 16 + kind * 8 + hop * 4 + which * 2 + way
         wait_recv(arriving(stage, kind, hop, which, way), ring_r.at[i])
+
+    def pass_on(kind, which, by, src=None):
+        j = mod((x, y)[which] + by, 4)
+        ref = (los[kind].at[c, yh, yl, j], his[kind].at[c, x, div(j, 2), mod(j, 2)])[which]
+        for way in range(2):
+            i = 16 + kind * 8 + which * 2 + way
+            dev = (ydev, xdev)[which](1 if way == 0 else 3)
+            rcopy(ref if src is None else src, ref, ring_s.at[i], ring_r.at[i], *dev).start()
 
     both = [(which, way) for which in range(2) for way in range(2)]
 
@@ -276,15 +291,18 @@
             ring_copy(0, kind, 0, which, way).start()
         for which in range(2):
             piece, me, dev = rings[0][which]
-            span = pl.ds(0, SPLIT) if which == 0 else pl.ds(SPLIT, NZ - SPLIT)
+            span = pl.ds(0, SPLITS[kind]) if which == 0 else pl.ds(SPLITS[kind], NZ - SPLITS[kind])
             copy = pltpu.make_async_copy(zunits[kind].at[span], piece(me, 0, kind), keep_s.at[kind * 2 + which])
             copy.start()
+            pass_on(kind, which, 0, zunits[kind].at[span])
             keeps.append(copy)
     turn_rows(1)
     for kind in range(2):
         for which, way in both:
             ring_arrived(0, kind, 0, which, way)
             ring_copy(0, kind, 1, which, way).start()
+        for which, way in both:
+            pass_on(kind, which, 3 if way == 0 else 1)
     for copy in keeps:
         copy.wait()
     turn_rows(2)
@@ -300,8 +318,8 @@
     for kind in range(2):
         for which, way in both:
             ring_arrived(0, kind, 1, which, way)
-        for which, way in both:
-            ring_copy(1, kind, 0, which, way).start()
+        for which in range(2):
+            pass_on(kind, which, 2)
     pack_rows(0)
     for kind in range(2):
         for which in range(2):
@@ -323,40 +341,56 @@
 
     last_hop(0)
 
-    for h in range(len(CHUNKS)):
+    def packed_chunk(h):
+        return p2rx[h][...].reshape(ROWS, CHUNKS[h][1])
+
+    def squares(h):
+        wide = packed_chunk(h).astype(F32)
+        return jnp.sum(wide * wide, axis=-1, keepdims=True)
+
+    def unit(kind, core, xx, zz, ys, cols):
+        if zz < SPLITS[kind]:
+            return los[kind][core, :, ys, xx, zz, :, cols]
+        return his[kind][core, xx, :, ys, zz - SPLITS[kind], :, cols]
+
+    def gate_rows(core, xx, t, cols, n):
+        parts = [unit(0, core, xx, zz, slice(None), cols).reshape(64, n) for zz in range(4 * t, 4 * t + 4)]
+        return jnp.concatenate(parts, axis=0)
+
+    def arrived_chunk(h):
         own2[h].wait()
         wait_recv(p2rx[h].at[pl.ds(0, PAGES - 1)], p2_r.at[h])
 
-    @pl.loop(0, 4)
-    def _(r):
-        rows = pl.ds(pl.multiple_of(r * 128, 128), 128)
-        mixed = [p2rx[h][pl.ds(r * 8, 8)].reshape(128, n).astype(F32) for h, (at, n) in enumerate(CHUNKS)]
-        total = sum(jnp.sum(v * v, axis=-1, keepdims=True) for v in mixed)
-        scale = lax.rsqrt(total / D + EPS)
-        for v, (at, n) in zip(mixed, CHUNKS):
-            ynorm[rows, at : at + n] = (v * scale).astype(BF)
-
     for copy in cores[0]:
         copy.wait_recv()
-
-    def unit(kind, core, xx, zz, ys):
-        if zz < SPLIT:
-            return los[kind][core, :, ys, xx, zz]
-        return his[kind][core, xx, :, ys, zz - SPLIT]
+    arrived_chunk(0)
+    arrived_chunk(1)
 
     @pl.loop(0, 4)
     def _(xx):
         for t in range(2):
-            zs = range(4 * t, 4 * t + 4)
-            rows = [
-                jnp.concatenate([unit(0, core, xx, zz, slice(None)).reshape(64, D) for zz in zs], axis=0)
+            cols = pl.ds(pl.multiple_of(xx * 512 + t * 256, 256), 256)
+            for core in range(2):
+                sums[core, :, cols] = sum(
+                    matmul_nt(packed_chunk(h), gate_rows(core, xx, t, slice(h * 256, h * 256 + 256), 256)) for h in range(2)
+                )
+
+    first_squares = squares(0) + squares(1)
+    last_hop(1)
+    arrived_chunk(2)
+    scale = lax.rsqrt((first_squares + squares(2)) / D + EPS)
+    scales[...] = jnp.broadcast_to(scale, (ROWS, 256))
+
+    @pl.loop(0, 4)
+    def _(xx):
+        for t in range(2):
+            cols = pl.ds(pl.multiple_of(xx * 512 + t * 256, 256), 256)
+            gate, up = [
+                (sums[core, :, cols] + matmul_nt(packed_chunk(2), gate_rows(core, xx, t, slice(512, D), 512))) * scales[...]
                 for core in range(2)
             ]
-            gate, up = matmul_nt(ynorm[...], rows[0]), matmul_nt(ynorm[...], rows[1])
-            cols = pl.ds(pl.multiple_of(xx * 512 + t * 256, 256), 256)
             hid[:, cols] = (gate / (1.0 + jnp.exp(-gate)) * up).astype(BF)
 
-    last_hop(1)
     for copy in cores[1]:
         copy.wait_recv()
 
@@ -364,7 +398,7 @@
         at = t * 256 - CHUNKS[h][0]
         total = p2rx[h][:, :, at : at + 256].reshape(ROWS, 256).astype(F32)
         for q in range(4):
-            down = jnp.concatenate([unit(1, q % 2, t, zz, q // 2).reshape(32, 512) for zz in range(NZ)], axis=0)
+            down = jnp.concatenate([unit(1, q % 2, t, zz, q // 2, slice(None)).reshape(32, 512) for zz in range(NZ)], axis=0)
             total = total + matmul_nt(hid[:, q * 512 : (q + 1) * 512], down)
         o_ref[:, t * 256 : (t + 1) * 256] = total.astype(BF)
 
@@ -410,16 +444,17 @@
             pltpu.VMEM((3, 16, 512), BF),
             pltpu.VMEM((NZ, 16, D), BF),
             pltpu.VMEM((NZ, 16, 512), BF),
-            pltpu.VMEM((NC, 2, 2, NX, SPLIT, 16, D), BF),
-            pltpu.VMEM((NC, NX, 2, 2, NZ - SPLIT, 16, D), BF),
-            pltpu.VMEM((NC, 2, 2, NX, SPLIT, 16, 512), BF),
-            pltpu.VMEM((NC, NX, 2, 2, NZ - SPLIT, 16, 512), BF),
+            pltpu.VMEM((NC, 2, 2, NX, SPLITS[0], 16, D), BF),
+            pltpu.VMEM((NC, NX, 2, 2, NZ - SPLITS[0], 16, D), BF),
+            pltpu.VMEM((NC, 2, 2, NX, SPLITS[1], 16, 512), BF),
+            pltpu.VMEM((NC, NX, 2, 2, NZ - SPLITS[1], 16, 512), BF),
             pltpu.VMEM((ROWS, D), BF),
             pltpu.VMEM((ROWS, ROWS), BF),
             pltpu.VMEM((ROWS, D), BF),
             pltpu.VMEM((ROWS, ROWS), BF),
             pltpu.VMEM((ROWS, ROWS), BF),
-            pltpu.VMEM((ROWS, D), BF),
+            pltpu.VMEM((2, ROWS, FF), F32),
+            pltpu.VMEM((ROWS, 256), F32),
             pltpu.VMEM((ROWS, FF), BF),
             *[[pltpu.VMEM((TOKS, 4, PER, n), BF) for at, n in CHUNKS] for k in range(2)],
             *[[pltpu.VMEM((PAGES, PER, n), BF) for at, n in CHUNKS] for k in range(4)],

time: 86.8 us -> 83.7 us (0.964)
  Pallas kernels: 84.4 us -> 81.3 us
    pallas_call x1, Pallas kernels: 84.4 us -> 81.3 us  [per_device(): pl.pallas_call(body, out_shape=jax.ShapeDtypeStruct((ROWS, D), BF), in_sp...]
where the time goes in v5:
time: 83.7 us; the launch traced here: 83.6 us
  Pallas kernels  81.3 us (97%)
  local copies, waits for them, and re-layouts  1.62 us (2%)
    pallas_call x1, Pallas kernels, per_device(): pl.pallas_call(body, out_shape=jax.ShapeDtypeStruct((ROWS, D), BF), in_sp...  81.3 us

profile of v5, /device:TPU:1, one launch (start us, length us, event | category | flops | bytes accessed | tf_op | source)
XLA Modules:
  0.0 83.6 jit_solution(17904180855049786073)
XLA Ops:
  0.7 0.0 copy-start
  0.7 0.6 copy-done
  1.3 81.3 %shard_map.73 = bf16[512,1024]{1,0:T(8,128)(2,1)S(1)} custom-call(s32[1]{0:T(128)S(6)} %copy.9.len_ref, s32[1,4]{1,0:T(1,128)S(1)} %copy-done, bf16[512,1024]{1,0:T(8,128)(2,1)} %bitcast.5, bf16[4,128,128]{2,1,0:T(8,128)(2,1)} %bm_hbm.1, bf16[16,32,32]{2,1,0:T(8,128)(2,1)} %sm_hbm.1, bf16[2,8,1024]{2,1,0:T(8,128)(2,1)} %bitcast.6, bf16[4,2048]{1,0:T(4,128)(2,1)} %bitcast.7), custom_call_target="tpu_custom_call" | custom-call | tf_op jit(solution)/shard_map/pallas_call | solution.py:429
  82.6 1.0 %copy.10 = bf16[1,512,1024]{2,1,0:T(8,128)(2,1)} copy(bf16[1,512,1024]{2,1,0:T(8,128)(2,1)S(1)} %bitcast.4) | data formatting | bytes 2097152
Async XLA Ops:
  0.7 0.7 copy-start

commit v6 on v5

--- a/solution.py
+++ b/solution.py
@@ -10,7 +10,7 @@
 ROWS, D, FF = 512, 1024, 2048
 BLK, NB, PER = 128, 32, 16
 EPS = 1e-05
-SPLITS = (5, 6)
+SPLITS = (6, 5)
 CHUNKS = ((0, 256), (256, 256), (512, 512))
 MESH = pl.DeviceIdType.MESH
 NT = (((1,), (1,)), ((), ()))

time: 83.7 us -> 82.2 us (0.982)
  Pallas kernels: 81.3 us -> 79.1 us
    pallas_call x1, Pallas kernels: 81.3 us -> 79.1 us  [per_device(): pl.pallas_call(body, out_shape=jax.ShapeDtypeStruct((ROWS, D), BF), in_sp...]
where the time goes in v6:
time: 82.2 us; the launch traced here: 81.4 us
  Pallas kernels  79.1 us (96%)
  local copies, waits for them, and re-layouts  1.62 us (2%)
    pallas_call x1, Pallas kernels, per_device(): pl.pallas_call(body, out_shape=jax.ShapeDtypeStruct((ROWS, D), BF), in_sp...  79.1 us

profile of v6, /device:TPU:1, one launch (start us, length us, event | category | flops | bytes accessed | tf_op | source)
XLA Modules:
  0.0 81.4 jit_solution(3140274210672474020)
XLA Ops:
  0.7 0.0 copy-start
  0.7 0.6 copy-done
  1.3 79.1 %shard_map.73 = bf16[512,1024]{1,0:T(8,128)(2,1)S(1)} custom-call(s32[1]{0:T(128)S(6)} %copy.9.len_ref, s32[1,4]{1,0:T(1,128)S(1)} %copy-done, bf16[512,1024]{1,0:T(8,128)(2,1)} %bitcast.5, bf16[4,128,128]{2,1,0:T(8,128)(2,1)} %bm_hbm.1, bf16[16,32,32]{2,1,0:T(8,128)(2,1)} %sm_hbm.1, bf16[2,8,1024]{2,1,0:T(8,128)(2,1)} %bitcast.6, bf16[4,2048]{1,0:T(4,128)(2,1)} %bitcast.7), custom_call_target="tpu_custom_call" | custom-call | tf_op jit(solution)/shard_map/pallas_call | solution.py:429
  80.4 1.0 %copy.10 = bf16[1,512,1024]{2,1,0:T(8,128)(2,1)} copy(bf16[1,512,1024]{2,1,0:T(8,128)(2,1)S(1)} %bitcast.4) | data formatting | bytes 2097152
Async XLA Ops:
  0.7 0.7 copy-start

commit v7 on v6

--- a/solution.py
+++ b/solution.py
@@ -43,8 +43,8 @@
 
 
 def body(
-    len_ref, occ_ref, x_hbm, bm_hbm, sm_hbm, wg_hbm, wd_hbm, o_ref,
-    x_ref, bm_ref, sm_ref, wg_ref, wd_ref,
+    len_ref, occ_hbm, x_hbm, bm_hbm, sm_hbm, wg_hbm, wd_hbm, o_ref,
+    occ_ref, x_ref, bm_ref, sm_ref, wg_ref, wd_ref,
     lens_rx, gu_tx, gu_rx, wd_tx, wd_rx, zunit_gu, zunit_wd, gu_lo, gu_hi, wd_lo, wd_hi, xm, spread, pre, psel, picks,
     sums, scales, hid,
     fsend, frecv, p1tx, p1rx, p2tx, p2rx,
@@ -72,7 +72,10 @@
     loads = [
         pltpu.make_async_copy(src, dst, in_s.at[i])
         for i, (src, dst) in enumerate(
-            [(wg_hbm, wg_ref), (wd_hbm, wd_ref), (x_hbm, x_ref), (bm_hbm, bm_ref), (sm_hbm, sm_ref)]
+            [
+                (wg_hbm, wg_ref), (wd_hbm, wd_ref), (x_hbm, x_ref), (bm_hbm, bm_ref), (sm_hbm, sm_ref),
+                (occ_hbm, occ_ref),
+            ]
         )
     ]
     for load in loads:
@@ -101,8 +104,9 @@
 
     loads[2].wait()
     loads[3].wait()
+    loads[5].wait()
     for b in range(4):
-        limit = length * occ_ref[0, b] - tok * ROWS - b * BLK
+        limit = length * occ_ref[:, b : b + 1] - tok * ROWS - b * BLK
         rows = slice(b * BLK, (b + 1) * BLK)
         live = iota((BLK, D), 0) < limit
         masked = jnp.where(live, x_ref[rows, :].astype(F32), 0.0)
@@ -429,9 +433,10 @@
     packed = pl.pallas_call(
         body,
         out_shape=jax.ShapeDtypeStruct((ROWS, D), BF),
-        in_specs=[smem, smem] + [anywhere] * 5,
+        in_specs=[smem] + [anywhere] * 6,
         out_specs=vmem,
         scratch_shapes=[
+            pltpu.VMEM((1, 4), jnp.int32),
             pltpu.VMEM((ROWS, D), BF),
             pltpu.VMEM((4, BLK, BLK), BF),
             pltpu.VMEM((PER, NB, NB), BF),
@@ -462,15 +467,15 @@
         + [dma] * 6
         + [dma((2,))] * 2
         + [dma((3,))] * 6
-        + [dma((32,)), dma((32,)), dma((20,)), dma((20,)), dma((9,)), dma((5,)), dma((4,)), dma((2,)), dma((2,))],
+        + [dma((32,)), dma((32,)), dma((20,)), dma((20,)), dma((9,)), dma((6,)), dma((4,)), dma((2,)), dma((2,))],
         compiler_params=pltpu.CompilerParams(
             collective_id=0, has_side_effects=True, vmem_limit_bytes=48 * 1024 * 1024
         ),
     )(
-        page_lengths, occupancy,
+        page_lengths,
         *(
             pltpu.with_memory_space_constraint(v, pltpu.HBM)
-            for v in (tile_tokens[0], block_mix, stride_mix, jnp.swapaxes(w_gate_up, 1, 2), w_down.T)
+            for v in (occupancy, tile_tokens[0], block_mix, stride_mix, jnp.swapaxes(w_gate_up, 1, 2), w_down.T)
         ),
     )
     return packed.reshape(1, ROWS, D)

time: 82.2 us -> 81.1 us (0.987)
  no operation moved by 1% of the time
where the time goes in v7:
time: 81.1 us; the launch traced here: 80.4 us
  Pallas kernels  78.7 us (97%)
  local copies, waits for them, and re-layouts  0.97 us (1%)
    pallas_call x1, Pallas kernels, per_device(): pl.pallas_call(body, out_shape=jax.ShapeDtypeStruct((ROWS, D), BF), in_sp...  78.7 us

profile of v7, /device:TPU:1, one launch (start us, length us, event | category | flops | bytes accessed | tf_op | source)
XLA Modules:
  0.0 80.4 jit_solution(12275791824386294514)
XLA Ops:
  0.7 78.7 %shard_map.73 = bf16[512,1024]{1,0:T(8,128)(2,1)S(1)} custom-call(s32[1]{0:T(128)S(6)} %copy.9.len_ref, s32[1,4]{1,0:T(1,128)} %occ_hbm.1, bf16[512,1024]{1,0:T(8,128)(2,1)} %bitcast.5, bf16[4,128,128]{2,1,0:T(8,128)(2,1)} %bm_hbm.1, bf16[16,32,32]{2,1,0:T(8,128)(2,1)} %sm_hbm.1, bf16[2,8,1024]{2,1,0:T(8,128)(2,1)} %bitcast.6, bf16[4,2048]{1,0:T(4,128)(2,1)} %bitcast.7), custom_call_target="tpu_custom_call" | custom-call | tf_op jit(solution)/shard_map/pallas_call | solution.py:433
  79.4 1.0 %copy.10 = bf16[1,512,1024]{2,1,0:T(8,128)(2,1)} copy(bf16[1,512,1024]{2,1,0:T(8,128)(2,1)S(1)} %bitcast.4) | data formatting | bytes 2097152
